TPU v7x, 256 devices: a whole 4x4x8 slice. The times are simulated.
256 devices in a mesh: val: 8 (over x_lo, y), col: 32 (over x_hi, z, core).
Axes of the slice: x: 4 (x_hi: 2, x_lo: 2; x = x_hi * 2 + x_lo), y: 4, z: 8, core: 2. Of those that a mesh axis runs over, the one named last changes fastest.
Arguments:
- valence_store: float32 [8, 32, 2, 48, 2304], P('val', 'col'), may hold values from -6 to 6
- band_owner: int32 [8], replicated, may hold values from 0 to 31
- valence_energy: float32 [8], P('val'), may hold values from -8 to -1
- cond_bands: float32 [128, 2, 48, 2304], P('col'), may hold values from -6 to 6
- cond_energy: float32 [128], P('col'), may hold values from 0.5 to 10
- gvec_index: int32 [4096], replicated, may hold values from 0 to 110591, as said below
Outputs:
- chi_zero: float32 [2, 512, 4096], P(None, 'val', 'col')
Inputs may be any that keep to these rules, and one draw needn't show every extreme that they name: `gvec_index`: distinct grid indices; entry 0 is 0 (the zero vector) and entry 1 is 110591.
All inputs are finite; a program needn't handle non-finite values.
Results may differ from a plain program's by a relative error of at most 0.0038.
Values may be sent and summed in bfloat16 or wider, within the bound.
No kernel may reach another device: no remote copies, remote signals or barrier semaphores. Data moves between devices by JAX's collectives and lax.ppermute only.
A program may use at most 256 MiB of HBM per device.

v0:
```python
import numpy as np

import jax
import jax.numpy as jnp
from jax import lax
from jax.experimental import pallas as pl
from jax.experimental.pallas import tpu as pltpu
from jax.sharding import PartitionSpec as P

ROW_DEV = 64
L = 48
YI = 8
YB = L // YI
SLAB = YI * L
R1 = YB * L
K1 = 6 * R1
K1P = 1792
K2 = 6 * SLAB
BF = jnp.bfloat16
F32 = jnp.float32


def tables():
    def trig(phase):
        angle = 2.0 * np.pi * (phase % L) / L
        return np.stack([np.cos(angle), np.sin(angle)]).astype(np.float32)

    r = np.arange(L)
    x_of = np.tile(r, YB)
    yb_of = np.repeat(np.arange(YB), L)
    t1a = trig(r[:, None] * x_of[None, :])
    t1b = trig(8 * np.arange(8)[:, None] * yb_of[None, :])
    ka_of = np.repeat(np.arange(YI), L)
    kz_of = np.tile(r, YI)
    t2a = trig(r[:, None] * kz_of[None, :])
    t2b = trig(6 * np.arange(YI)[:, None] * ka_of[None, :])
    yi_of = np.repeat(np.arange(YI), L)
    tw = trig(np.arange(8)[:, None] * yi_of[None, :])
    return t1a, t1b, t2a, t2b, tw


def split(value):
    hi = value.astype(BF)
    return hi, (value - hi.astype(F32)).astype(BF)


def pairs_kernel(word, v_ref, c_ref, scale_ref, t1a, t1b, t2a, t2b, tw, out_ref, a1, b2, p3, z1, l2, y2, grid):
    step = pl.program_id(0)

    @pl.when(step == 0)
    def _():
        a1[:, K1:K1P] = jnp.zeros((2 * R1, K1P - K1), BF)
        p3[K1:K1P, :] = jnp.zeros((K1P - K1, 2 * SLAB), BF)
        for kb in range(YB):
            cb = t1b[0, kb:kb + 1, :]
            sb = t1b[1, kb:kb + 1, :]
            cos = t1a[0] * cb - t1a[1] * sb
            sin = t1a[1] * cb + t1a[0] * sb
            top = jnp.concatenate([cos, sin], 1)
            low = jnp.concatenate([-sin, cos], 1)
            for ri, value in enumerate((top, low)):
                hi, lo = split(value)
                r0 = ri * R1 + kb * L
                a1[r0:r0 + L, 0:2 * R1] = hi
                a1[r0:r0 + L, 2 * R1:4 * R1] = lo
                a1[r0:r0 + L, 4 * R1:6 * R1] = hi
        for yi in range(YI):
            cb = t2b[0, yi:yi + 1, :]
            sb = t2b[1, yi:yi + 1, :]
            cos = t2a[0] * cb - t2a[1] * sb
            sin = t2a[1] * cb + t2a[0] * sb
            for ri, value in enumerate((jnp.concatenate([cos, -sin], 1), jnp.concatenate([sin, cos], 1))):
                hi, lo = split(value)
                r0 = ri * SLAB + yi * L
                b2[r0:r0 + L, :] = hi
                b2[2 * SLAB + r0:2 * SLAB + r0 + L, :] = lo
                b2[4 * SLAB + r0:4 * SLAB + r0 + L, :] = hi

    for yb in range(YB):
        lanes = slice(yb * SLAB, (yb + 1) * SLAB)
        v0 = v_ref[0, :, lanes]
        v1 = v_ref[1, :, lanes]
        for bb in range(2):
            c0 = c_ref[bb, 0, :, lanes]
            c1 = c_ref[bb, 1, :, lanes]
            for ri, value in enumerate((v0 * c0 + v1 * c1, v0 * c1 - v1 * c0)):
                hi, lo = split(value)
                r0 = ri * R1 + yb * L
                cols = slice(bb * SLAB, (bb + 1) * SLAB)
                p3[r0:r0 + L, cols] = hi
                p3[2 * R1 + r0:2 * R1 + r0 + L, cols] = hi
                p3[4 * R1 + r0:4 * R1 + r0 + L, cols] = lo
    z1[...] = jnp.dot(a1[...], p3[...], preferred_element_type=F32)
    for kb in range(YB):
        cw = tw[0, kb:kb + 1, :]
        sw = tw[1, kb:kb + 1, :]
        for bb in range(2):
            cols = slice(bb * SLAB, (bb + 1) * SLAB)
            zr = z1[kb * L:kb * L + L, cols]
            zi = z1[R1 + kb * L:R1 + kb * L + L, cols]
            rows = slice(bb * R1 + kb * L, bb * R1 + kb * L + L)
            for ri, value in enumerate((zr * cw + zi * sw, zi * cw - zr * sw)):
                hi, lo = split(value)
                l2[rows, ri * SLAB:(ri + 1) * SLAB] = hi
                l2[rows, (2 + ri) * SLAB:(3 + ri) * SLAB] = hi
                l2[rows, (4 + ri) * SLAB:(5 + ri) * SLAB] = lo
    y2[...] = jnp.dot(l2[...], b2[...], preferred_element_type=F32)
    for bb in range(2):
        for ri in range(2):
            for t in range(3):
                c0 = ri * SLAB + t * 128
                start = t * 8 + ri * 4 + bb + 2 * step
                grid[pl.ds(start, R1, stride=24), :] = y2[bb * R1:(bb + 1) * R1, c0:c0 + 128]

    @pl.when(step == 1)
    def _():
        lane = lax.broadcasted_iota(jnp.int32, (8, 128), 1)
        scale = scale_ref[...]

        def block(p, carry):
            outs = []
            for h in range(2):
                accs = [jnp.zeros((8, 128), F32) for _ in range(4)]
                for i in range(128):
                    w = word[(2 * p + h) * 128 + i]
                    start = pl.multiple_of((w >> 7) * 8, 8)
                    row = pltpu.roll(grid[pl.ds(start, 8), :], w & 127, 1)
                    accs[i % 4] = jnp.where(lane == i, row, accs[i % 4])
                outs.append(((accs[0] + accs[1]) + (accs[2] + accs[3])) * scale)
            out_ref[pl.ds(pl.multiple_of(p * 16, 16), 16), :] = jnp.concatenate(outs, 0).astype(BF)
            return carry

        lax.fori_loop(0, out_ref.shape[0] // 16, block, 0)


def pair_elements(valence, cond, scale, words):
    count = words.shape[0]
    rows = count // 128 * 8
    full = lambda *shape: pl.BlockSpec(shape, lambda s, w: (0,) * len(shape))
    consts = tables()
    return pl.pallas_call(
        pairs_kernel,
        out_shape=jax.ShapeDtypeStruct((rows, 128), BF),
        grid_spec=pltpu.PrefetchScalarGridSpec(
            num_scalar_prefetch=1,
            grid=(2,),
            in_specs=[
                full(2, L, L * L),
                pl.BlockSpec((2, 2, L, L * L), lambda s, w: (s, 0, 0, 0)),
                full(8, 128),
            ] + [full(*c.shape) for c in consts],
            out_specs=full(rows, 128),
            scratch_shapes=[
                pltpu.VMEM((2 * R1, K1P), BF),
                pltpu.VMEM((K2, 2 * SLAB), BF),
                pltpu.VMEM((K1P, 2 * SLAB), BF),
                pltpu.VMEM((2 * R1, 2 * SLAB), F32),
                pltpu.VMEM((2 * R1, K2), BF),
                pltpu.VMEM((2 * R1, 2 * SLAB), F32),
                pltpu.VMEM((R1 * 24, 128), F32),
            ],
        ),
        compiler_params=pltpu.CompilerParams(
            dimension_semantics=("arbitrary",), vmem_limit_bytes=50 << 20
        ),
        name="pairs",
    )(words, valence, cond, scale, *[jnp.asarray(c) for c in consts])


def gather_words(gvec_index):
    kx = gvec_index // (L * L)
    ky = gvec_index // L % L
    kz = gvec_index % L
    lane = ky // YB * L + kz
    tile = (ky % YB * L + kx) * 3 + lane // 128
    place = lax.iota(jnp.int32, gvec_index.shape[0])
    return tile * 128 + (place - lane) % 128


def local(valence_store, band_owner, valence_energy, cond_bands, cond_energy, gvec_index):
    n_col = lax.axis_size("col")
    n_val = lax.axis_size("val")
    chips = n_col // 2
    me = lax.axis_index("col")
    core = me % 2
    owner = band_owner[lax.axis_index("val")]

    tiles = valence_store[0, 0].astype(jnp.float16).reshape(2, 6, 8, 18, 128)
    tiles = tiles.transpose(0, 1, 3, 2, 4).reshape(2, 108, 8, 128)
    tiles = jnp.pad(tiles, ((0, 0), (0, 4), (0, 0), (0, 0)))
    swap = [(i, i ^ 1) for i in range(n_col)]
    mine = lax.dynamic_index_in_dim(tiles, core, 0, False)
    theirs = lax.dynamic_index_in_dim(tiles, 1 - core, 0, False)
    other = lax.ppermute(theirs, "col", swap)
    half = jnp.where(owner % 2 == core, mine, other)
    groups = [[q * 2 + c for q in range(chips)] for c in range(2)]
    got = lax.all_to_all(half.reshape(chips, 7, 8, 128), "col", 0, 0, tiled=True, axis_index_groups=groups)
    chunk = lax.dynamic_index_in_dim(got, owner // 2, 0, True)
    again = jnp.broadcast_to(chunk, (chips, 7, 8, 128))
    half = lax.all_to_all(again, "col", 0, 0, tiled=True, axis_index_groups=groups).reshape(112, 8, 128)
    other = lax.ppermute(half, "col", swap)
    both = jnp.stack([jnp.where(core == 0, half, other), jnp.where(core == 0, other, half)], 0)
    valence = both[:, :108].reshape(2, 6, 18, 8, 128).transpose(0, 1, 3, 2, 4).reshape(2, L, L * L).astype(F32)

    total_bands = cond_bands.shape[0] * n_col * n_val
    constant = total_bands ** (-0.25) * L ** (-1.5)
    scaling = jnp.sqrt(2.0 / (cond_energy - valence_energy[0])) * constant
    scale = jnp.broadcast_to(jnp.concatenate([scaling, scaling])[:, None], (8, 128))
    pairs = pair_elements(valence, cond_bands, scale, gather_words(gvec_index)).reshape(n_col, 8, 128)

    row_count = ROW_DEV * n_val
    row_blocks = row_count // 128
    heads = jnp.broadcast_to(pairs[None, :row_blocks], (n_col, row_blocks, 8, 128))
    sent = jnp.concatenate([pairs[:, None], heads], 1)
    came = lax.all_to_all(sent, "col", 0, 0, tiled=True)
    col = came[:, 0]
    turned = jnp.concatenate([-col[:, 4:], col[:, :4]], 1)
    right = jnp.concatenate([col, turned], 2).reshape(n_col * 8, 256)
    left = came[:, 1:].transpose(1, 0, 2, 3).reshape(row_blocks, n_col * 8, 128)
    part = -lax.dot_general(
        left, right, (((1,), (0,)), ((), ())), preferred_element_type=F32
    )
    part = part.reshape(n_val, ROW_DEV, 256).astype(BF)
    summands = lax.all_to_all(part, "val", 0, 0, tiled=True)
    total = jnp.sum(summands.astype(F32), 0)
    return total.reshape(ROW_DEV, 2, 128).transpose(1, 0, 2)


def solution(mesh):
    return jax.shard_map(
        local,
        mesh=mesh,
        in_specs=(
            P("val", "col", None, None, None),
            P(),
            P("val"),
            P("col", None, None, None),
            P("col"),
            P(),
        ),
        out_specs=P(None, "val", "col"),
        check_vma=False,
    )
```

profile of v0, /device:TPU:32, one launch (start us, length us, event | category | flops | bytes accessed | tf_op | source)
XLA Modules:
  0.0 100.9 jit_solution(13896086975267258025)
XLA Ops:
  0.0 0.0 copy-start.6
  0.0 0.0 copy-start.5
  0.0 0.0 copy-start
  0.0 0.0 copy-start.1
  0.0 0.0 copy-start.2
  0.0 0.0 copy-start.3
  0.0 0.0 copy-start.4
  0.1 1.3 %convert_element_type.27 = f16[1,1,2,48,2304]{4,3,2,1,0:T(8,128)(2,1)S(1)} convert(f32[1,1,2,48,2304]{4,3,2,1,0:T(8,128)} %param.11) | non-fusion elementwise | flops 221184 | bytes 1327104 | tf_op jit(solution)/shard_map/convert_element_type | solution.py:188
  1.4 0.1 fusion.4
  1.4 0.1 collective-permute-start
  1.6 1.2 %dynamic_slice.14 = s32[1]{0:T(128)} dynamic-slice(s32[8]{0:T(128)} %param.12, s32[]{:T(128)S(6)} %select_n.89), dynamic_slice_sizes={1} | dynamic-slice | bytes 12 | tf_op jit(solution)/shard_map/dynamic_slice | solution.py:186
  4.8 0.0 collective-permute-done
  4.8 0.8 fusion.3
  5.6 11.0 %all-to-all-start = ((f16[16,7,8,128]{3,2,1,0:T(8,128)(2,1)}), f16[16,7,8,128]{3,2,1,0:T(8,128)(2,1)S(1)}, u32[]{:S(2)}, u32[]{:S(2)}) async-start(f16[16,7,8,128]{3,2,1,0:T(8,128)(2,1)} %bitcast.6), calls=%async_computation | async-start | bytes 458752 | tf_op jit(solution)/shard_map/all_to_all | solution.py:197
  17.3 11.1 %all-to-all-done = f16[16,7,8,128]{3,2,1,0:T(8,128)(2,1)S(1)} async-done(((f16[16,7,8,128]{3,2,1,0:T(8,128)(2,1)}), f16[16,7,8,128]{3,2,1,0:T(8,128)(2,1)S(1)}, u32[]{:S(2)}, u32[]{:S(2)}) %all-to-all-start) | async-done | bytes 229408 | tf_op jit(solution)/shard_map/all_to_all | solution.py:197
  28.3 0.7 broadcast_in_dim.22
  29.1 4.4 %all-to-all-start.1 = ((f16[16,7,8,128]{3,2,1,0:T(8,128)(2,1)}), f16[16,7,8,128]{3,2,1,0:T(8,128)(2,1)S(1)}, u32[]{:S(2)}, u32[]{:S(2)}) async-start(f16[16,7,8,128]{3,2,1,0:T(8,128)(2,1)} %broadcast_in_dim.22), calls=%async_computation.1 | async-start | bytes 458752 | tf_op jit(solution)/shard_map/all_to_all | solution.py:200
  34.1 0.0 copy-done.6
  34.1 10.3 %all-to-all-done.1 = f16[16,7,8,128]{3,2,1,0:T(8,128)(2,1)S(1)} async-done(((f16[16,7,8,128]{3,2,1,0:T(8,128)(2,1)}), f16[16,7,8,128]{3,2,1,0:T(8,128)(2,1)S(1)}, u32[]{:S(2)}, u32[]{:S(2)}) %all-to-all-start.1) | async-done | bytes 229408 | tf_op jit(solution)/shard_map/all_to_all | solution.py:200
  44.4 0.0 collective-permute-start.1
  44.4 0.1 pad_maximum_fusion.2
  44.5 0.0 copy-done.5
  44.5 0.1 fusion.15.word
  44.6 1.3 %collective-permute-done.1 = f16[112,8,128]{2,1,0:T(8,128)(2,1)S(1)} collective-permute-done((f16[112,8,128]{2,1,0:T(8,128)(2,1)S(1)}, f16[112,8,128]{2,1,0:T(8,128)(2,1)S(1)}, u32[]{:S(2)}, u32[]{:S(2)}) %collective-permute-start.1) | collective-permute-done | bytes 229408 | tf_op jit(solution)/shard_map/ppermute | solution.py:201
  45.9 0.1 select_bitcast_fusion.1
  46.0 0.1 pad_maximum_fusion
  46.1 0.1 convert_bitcast_fusion.v_ref
  46.2 0.1 broadcast_in_dim.23.scale_ref
  46.3 0.0 copy-done
  46.3 0.0 copy-done.1
  46.3 0.0 copy-done.2
  46.3 0.0 copy-done.3
  46.3 0.0 copy-done.4
  46.3 22.5 %pairs.1 = bf16[256,128]{1,0:T(8,128)(2,1)S(1)} custom-call(s32[4096]{0:T(1024)S(1)} %fusion.15.word, f32[2,48,2304]{2,1,0:T(8,128)S(1)} %convert_bitcast_fusion.v_ref, f32[4,2,48,2304]{3,2,1,0:T(8,128)} %c_ref.1, f32[8,128]{1,0:T(8,128)S(1)} %broadcast_in_dim.23.scale_ref, f32[2,48,288]{2,1,0:T(8,128)S(1)} %copy-done, f32[2,8,288]{2,1,0:T(8,128)S(1)} %copy-done.2, ...), custom_call_target="tpu_custom_call" | custom-call | tf_op jit(solution)/shard_map/pairs/pallas_call | solution.py:141
  68.9 19.4 %all_to_all.20 = bf16[32,5,8,128]{3,2,1,0:T(8,128)(2,1)S(1)} all-to-all(bf16[32,5,8,128]{3,2,1,0:T(8,128)(2,1)S(1)} %pad_maximum_fusion.1), channel_id=1, replica_groups=mesh['val'=8,'col'=32] {'col'}, dimensions={0} | all-to-all | bytes 655360 | tf_op jit(solution)/shard_map/all_to_all | solution.py:215
  88.3 0.3 fusion.1
  88.6 11.5 %all_to_all.21 = bf16[8,64,256]{2,1,0:T(8,128)(2,1)S(1)} all-to-all(bf16[8,64,256]{2,1,0:T(8,128)(2,1)S(1)} %bitcast.58), channel_id=1, replica_groups=mesh['val'=8,'col'=32] {'val'}, dimensions={0} | all-to-all | bytes 524288 | tf_op jit(solution)/shard_map/all_to_all | solution.py:224
  100.2 0.6 copy.18
  (11 shorter events, 0.2 us)
Async XLA Ops:
  0.0 34.1 %copy-start.6 = (f32[4]{0:T(128)S(1)}, f32[4]{0:T(128)}, u32[]{:S(2)}) copy-start(f32[4]{0:T(128)} %param.15) | copy-start | bytes 52
  0.0 44.5 %copy-start.5 = (s32[4096]{0:T(1024)S(1)}, s32[4096]{0:T(1024)}, u32[]{:S(2)}) copy-start(s32[4096]{0:T(1024)} %param.16) | copy-start | bytes 49156
  0.0 46.3 %copy-start = (f32[2,48,288]{2,1,0:T(8,128)S(1)}, f32[2,48,288]{2,1,0:T(8,128)}, u32[]{:S(2)}) copy-start(f32[2,48,288]{2,1,0:T(8,128)} %constant.133.clone.t1a) | copy-start | bytes 331780
  0.0 46.3 %copy-start.1 = (f32[2,48,384]{2,1,0:T(8,128)S(1)}, f32[2,48,384]{2,1,0:T(8,128)}, u32[]{:S(2)}) copy-start(f32[2,48,384]{2,1,0:T(8,128)} %constant.135.clone.t2a) | copy-start | bytes 442372
  0.0 46.3 %copy-start.2 = (f32[2,8,288]{2,1,0:T(8,128)S(1)}, f32[2,8,288]{2,1,0:T(8,128)}, u32[]{:S(2)}) copy-start(f32[2,8,288]{2,1,0:T(8,128)} %constant.134.clone.t1b) | copy-start | bytes 55300
  0.0 46.3 %copy-start.3 = (f32[2,8,384]{2,1,0:T(8,128)S(1)}, f32[2,8,384]{2,1,0:T(8,128)}, u32[]{:S(2)}) copy-start(f32[2,8,384]{2,1,0:T(8,128)} %constant.136.clone.t2b) | copy-start | bytes 73732
  0.0 46.3 %copy-start.4 = (f32[2,8,384]{2,1,0:T(8,128)S(1)}, f32[2,8,384]{2,1,0:T(8,128)}, u32[]{:S(2)}) copy-start(f32[2,8,384]{2,1,0:T(8,128)} %constant.137.clone.tw) | copy-start | bytes 73732
  1.4 3.3 %collective-permute-start = (f16[112,8,128]{2,1,0:T(8,128)(2,1)S(1)}, f16[112,8,128]{2,1,0:T(8,128)(2,1)S(1)}, u32[]{:S(2)}, u32[]{:S(2)}) collective-permute-start(f16[112,8,128]{2,1,0:T(8,128)(2,1)S(1)} %fusion.4), channel_id=1, source_target_pairs={{0,1},{1,0},{2,3},{3,2},{4,5},{5,4},{6,7},{7,6},{8,9},{9,8},{10,11... | collective-permute-start | bytes 688136 | tf_op jit(solution)/shard_map/ppermute | solution.py:194
  5.6 22.8 %all-to-all-start = ((f16[16,7,8,128]{3,2,1,0:T(8,128)(2,1)}), f16[16,7,8,128]{3,2,1,0:T(8,128)(2,1)S(1)}, u32[]{:S(2)}, u32[]{:S(2)}) async-start(f16[16,7,8,128]{3,2,1,0:T(8,128)(2,1)} %bitcast.6), calls=%async_computation | async-start | bytes 458752 | tf_op jit(solution)/shard_map/all_to_all | solution.py:197
  29.1 15.3 %all-to-all-start.1 = ((f16[16,7,8,128]{3,2,1,0:T(8,128)(2,1)}), f16[16,7,8,128]{3,2,1,0:T(8,128)(2,1)S(1)}, u32[]{:S(2)}, u32[]{:S(2)}) async-start(f16[16,7,8,128]{3,2,1,0:T(8,128)(2,1)} %broadcast_in_dim.22), calls=%async_computation.1 | async-start | bytes 458752 | tf_op jit(solution)/shard_map/all_to_all | solution.py:200
  44.4 1.5 %collective-permute-start.1 = (f16[112,8,128]{2,1,0:T(8,128)(2,1)S(1)}, f16[112,8,128]{2,1,0:T(8,128)(2,1)S(1)}, u32[]{:S(2)}, u32[]{:S(2)}) collective-permute-start(f16[112,8,128]{2,1,0:T(8,128)(2,1)S(1)} %bitcast.57), channel_id=1, source_target_pairs={{0,1},{1,0},{2,3},{3,2},{4,5},{5,4},{6,7},{7,6},{8,9},{9,8},{10,11... | collective-permute-start | bytes 688136 | tf_op jit(solution)/shard_map/ppermute | solution.py:201
where the time goes:
time: 102 us; the launch traced here: 101 us
  blocking collectives  30.9 us (30%)
  waiting for transfers between devices  22.7 us (22%)
  Pallas kernels  22.5 us (22%)
  starting transfers between devices  15.5 us (15%)
  between operations  3.49 us (3%)
  local copies, waits for them, and re-layouts  2.9 us (3%)
  other arithmetic  2.67 us (3%)
    pallas_call x1, Pallas kernels, pair_elements(): pl.pallas_call(pairs_kernel, out_shape=jax.ShapeDtypeStruct((rows, 128),...  22.5 us
    all_to_all x1, blocking collectives, local(): came = lax.all_to_all(sent, 'col', 0, 0, tiled=True)  19.4 us
    all_to_all x1, blocking collectives, local(): summands = lax.all_to_all(part, 'val', 0, 0, tiled=True)  11.5 us
    all_to_all x1, waiting for transfers between devices, local(): lax.all_to_all(half.reshape(chips, 7, 8, 128), 'col', 0, 0, tiled=True, a...  11.1 us
    all_to_all x1, starting transfers between devices, local(): lax.all_to_all(half.reshape(chips, 7, 8, 128), 'col', 0, 0, tiled=True, a...  11 us
    all_to_all x1, waiting for transfers between devices, local(): lax.all_to_all(again, 'col', 0, 0, tiled=True, axis_index_groups=groups)  10.3 us
    all_to_all x1, starting transfers between devices, local(): lax.all_to_all(again, 'col', 0, 0, tiled=True, axis_index_groups=groups)  4.35 us
  transfers between devices with their start and end apart: 4, of which 3 were waited for; matrix products, arithmetic and copies ran while one was open for 1% of the time, Pallas kernels for 0%

commit v1 on v0

--- a/solution.py
+++ b/solution.py
@@ -13,9 +13,9 @@
 YB = L // YI
 SLAB = YI * L
 R1 = YB * L
-K1 = 6 * R1
-K1P = 1792
+K1 = 6 * L
 K2 = 6 * SLAB
+ROOT = 0.75 ** 0.5
 BF = jnp.bfloat16
 F32 = jnp.float32
 
@@ -26,17 +26,15 @@
         return np.stack([np.cos(angle), np.sin(angle)]).astype(np.float32)
 
     r = np.arange(L)
-    x_of = np.tile(r, YB)
-    yb_of = np.repeat(np.arange(YB), L)
-    t1a = trig(r[:, None] * x_of[None, :])
-    t1b = trig(8 * np.arange(8)[:, None] * yb_of[None, :])
     ka_of = np.repeat(np.arange(YI), L)
     kz_of = np.tile(r, YI)
+    t1 = trig(r[:, None] * r[None, :])
+    t1 = np.block([[t1[0], t1[1]], [-t1[1], t1[0]]])
     t2a = trig(r[:, None] * kz_of[None, :])
     t2b = trig(6 * np.arange(YI)[:, None] * ka_of[None, :])
     yi_of = np.repeat(np.arange(YI), L)
     tw = trig(np.arange(8)[:, None] * yi_of[None, :])
-    return t1a, t1b, t2a, t2b, tw
+    return t1, t2a, t2b, tw
 
 
 def split(value):
@@ -44,93 +42,105 @@
     return hi, (value - hi.astype(F32)).astype(BF)
 
 
-def pairs_kernel(word, v_ref, c_ref, scale_ref, t1a, t1b, t2a, t2b, tw, out_ref, a1, b2, p3, z1, l2, y2, grid):
+def dft3(s):
+    (r0, i0), (r1, i1), (r2, i2) = s
+    tr, ti = r1 + r2, i1 + i2
+    ur, ui = r0 - 0.5 * tr, i0 - 0.5 * ti
+    dr, di = (r1 - r2) * ROOT, (i1 - i2) * ROOT
+    return [(r0 + tr, i0 + ti), (ur + di, ui - dr), (ur - di, ui + dr)]
+
+
+def dft6(p):
+    a = [(p[m][0] + p[m + 3][0], p[m][1] + p[m + 3][1]) for m in range(3)]
+    b = [(p[m][0] - p[m + 3][0], p[m][1] - p[m + 3][1]) for m in range(3)]
+    b[1] = (p[4][0] - p[1][0], p[4][1] - p[1][1])
+    even = dft3(a)
+    odd = dft3(b)
+    return [even[0], odd[2], even[1], odd[0], even[2], odd[1]]
+
+
+def pairs_kernel(word, v_ref, c_ref, scale_ref, t1, t2a, t2b, tw, out_ref, a1, b2, p3, l2, grid):
     step = pl.program_id(0)
 
     @pl.when(step == 0)
     def _():
-        a1[:, K1:K1P] = jnp.zeros((2 * R1, K1P - K1), BF)
-        p3[K1:K1P, :] = jnp.zeros((K1P - K1, 2 * SLAB), BF)
-        for kb in range(YB):
-            cb = t1b[0, kb:kb + 1, :]
-            sb = t1b[1, kb:kb + 1, :]
-            cos = t1a[0] * cb - t1a[1] * sb
-            sin = t1a[1] * cb + t1a[0] * sb
-            top = jnp.concatenate([cos, sin], 1)
-            low = jnp.concatenate([-sin, cos], 1)
-            for ri, value in enumerate((top, low)):
-                hi, lo = split(value)
-                r0 = ri * R1 + kb * L
-                a1[r0:r0 + L, 0:2 * R1] = hi
-                a1[r0:r0 + L, 2 * R1:4 * R1] = lo
-                a1[r0:r0 + L, 4 * R1:6 * R1] = hi
+        hi, lo = split(t1[...])
+        a1[:, 0:2 * L] = hi
+        a1[:, 2 * L:4 * L] = lo
+        a1[:, 4 * L:6 * L] = hi
         for yi in range(YI):
             cb = t2b[0, yi:yi + 1, :]
             sb = t2b[1, yi:yi + 1, :]
             cos = t2a[0] * cb - t2a[1] * sb
             sin = t2a[1] * cb + t2a[0] * sb
-            for ri, value in enumerate((jnp.concatenate([cos, -sin], 1), jnp.concatenate([sin, cos], 1))):
+            for value, negative, spots in ((cos, False, ((0, 0), (1, 1))), (sin, True, ((1, 0), (0, 1)))):
                 hi, lo = split(value)
-                r0 = ri * SLAB + yi * L
-                b2[r0:r0 + L, :] = hi
-                b2[2 * SLAB + r0:2 * SLAB + r0 + L, :] = lo
-                b2[4 * SLAB + r0:4 * SLAB + r0 + L, :] = hi
-
-    for yb in range(YB):
-        lanes = slice(yb * SLAB, (yb + 1) * SLAB)
-        v0 = v_ref[0, :, lanes]
-        v1 = v_ref[1, :, lanes]
-        for bb in range(2):
-            c0 = c_ref[bb, 0, :, lanes]
-            c1 = c_ref[bb, 1, :, lanes]
-            for ri, value in enumerate((v0 * c0 + v1 * c1, v0 * c1 - v1 * c0)):
-                hi, lo = split(value)
-                r0 = ri * R1 + yb * L
-                cols = slice(bb * SLAB, (bb + 1) * SLAB)
-                p3[r0:r0 + L, cols] = hi
-                p3[2 * R1 + r0:2 * R1 + r0 + L, cols] = hi
-                p3[4 * R1 + r0:4 * R1 + r0 + L, cols] = lo
-    z1[...] = jnp.dot(a1[...], p3[...], preferred_element_type=F32)
+                for ri, half in spots:
+                    flip = negative and ri == 0
+                    high, low = (-hi, -lo) if flip else (hi, lo)
+                    cols = slice(half * SLAB, (half + 1) * SLAB)
+                    r0 = ri * SLAB + yi * L
+                    b2[r0:r0 + L, cols] = high
+                    b2[2 * SLAB + r0:2 * SLAB + r0 + L, cols] = low
+                    b2[4 * SLAB + r0:4 * SLAB + r0 + L, cols] = high
+
+    for lt in range(SLAB // 128):
+        for xc in range(L // 16):
+            xs = slice(xc * 16, xc * 16 + 16)
+            for bb in range(2):
+                cols = slice(bb * SLAB + lt * 128, bb * SLAB + lt * 128 + 128)
+                p = []
+                for yb in range(YB):
+                    lanes = slice(yb * SLAB + lt * 128, yb * SLAB + lt * 128 + 128)
+                    v0 = v_ref[0, xs, lanes]
+                    v1 = v_ref[1, xs, lanes]
+                    c0 = c_ref[bb, 0, xs, lanes]
+                    c1 = c_ref[bb, 1, xs, lanes]
+                    p.append((v0 * c0 + v1 * c1, v0 * c1 - v1 * c0))
+                for kb, q in enumerate(dft6(p)):
+                    for ri in range(2):
+                        hi, lo = split(q[ri])
+                        r0 = ri * L + xc * 16
+                        p3[kb, r0:r0 + 16, cols] = hi
+                        p3[kb, 2 * L + r0:2 * L + r0 + 16, cols] = hi
+                        p3[kb, 4 * L + r0:4 * L + r0 + 16, cols] = lo
     for kb in range(YB):
+        z = jnp.dot(a1[...], p3[kb], preferred_element_type=F32)
         cw = tw[0, kb:kb + 1, :]
         sw = tw[1, kb:kb + 1, :]
         for bb in range(2):
-            cols = slice(bb * SLAB, (bb + 1) * SLAB)
-            zr = z1[kb * L:kb * L + L, cols]
-            zi = z1[R1 + kb * L:R1 + kb * L + L, cols]
+            zr = z[:L, bb * SLAB:(bb + 1) * SLAB]
+            zi = z[L:, bb * SLAB:(bb + 1) * SLAB]
             rows = slice(bb * R1 + kb * L, bb * R1 + kb * L + L)
             for ri, value in enumerate((zr * cw + zi * sw, zi * cw - zr * sw)):
                 hi, lo = split(value)
                 l2[rows, ri * SLAB:(ri + 1) * SLAB] = hi
                 l2[rows, (2 + ri) * SLAB:(3 + ri) * SLAB] = hi
                 l2[rows, (4 + ri) * SLAB:(5 + ri) * SLAB] = lo
-    y2[...] = jnp.dot(l2[...], b2[...], preferred_element_type=F32)
+    y = jnp.dot(l2[...], b2[...], preferred_element_type=F32)
     for bb in range(2):
         for ri in range(2):
             for t in range(3):
                 c0 = ri * SLAB + t * 128
                 start = t * 8 + ri * 4 + bb + 2 * step
-                grid[pl.ds(start, R1, stride=24), :] = y2[bb * R1:(bb + 1) * R1, c0:c0 + 128]
-
-    @pl.when(step == 1)
-    def _():
-        lane = lax.broadcasted_iota(jnp.int32, (8, 128), 1)
-        scale = scale_ref[...]
-
-        def block(p, carry):
-            outs = []
-            for h in range(2):
-                accs = [jnp.zeros((8, 128), F32) for _ in range(4)]
-                for i in range(128):
-                    w = word[(2 * p + h) * 128 + i]
-                    start = pl.multiple_of((w >> 7) * 8, 8)
-                    row = pltpu.roll(grid[pl.ds(start, 8), :], w & 127, 1)
-                    accs[i % 4] = jnp.where(lane == i, row, accs[i % 4])
-                outs.append(((accs[0] + accs[1]) + (accs[2] + accs[3])) * scale)
-            out_ref[pl.ds(pl.multiple_of(p * 16, 16), 16), :] = jnp.concatenate(outs, 0).astype(BF)
-            return carry
-
-        lax.fori_loop(0, out_ref.shape[0] // 16, block, 0)
+                grid[pl.ds(start, R1, stride=24), :] = y[bb * R1:(bb + 1) * R1, c0:c0 + 128]
+
+    lane = lax.broadcasted_iota(jnp.int32, (8, 128), 1)
+
+    def block(p):
+        outs = []
+        for h in range(2):
+            accs = [jnp.zeros((8, 128), F32) for _ in range(4)]
+            for i in range(128):
+                w = word[(2 * p + h) * 128 + i]
+                start = pl.multiple_of(w >> 7, 8)
+                row = pltpu.roll(grid[pl.ds(start, 8), :], w & 127, 1)
+                accs[i % 4] = jnp.where(lane == i, row, accs[i % 4])
+            outs.append(((accs[0] + accs[1]) + (accs[2] + accs[3])) * scale_ref[...])
+        out_ref[p * 16:p * 16 + 16, :] = jnp.concatenate(outs, 0).astype(BF)
+
+    for p in range(out_ref.shape[0] // 16):
+        pl.when(step == 1)(lambda p=p: block(p))
 
 
 def pair_elements(valence, cond, scale, words):
@@ -151,12 +161,10 @@
             ] + [full(*c.shape) for c in consts],
             out_specs=full(rows, 128),
             scratch_shapes=[
-                pltpu.VMEM((2 * R1, K1P), BF),
+                pltpu.VMEM((2 * L, K1), BF),
                 pltpu.VMEM((K2, 2 * SLAB), BF),
-                pltpu.VMEM((K1P, 2 * SLAB), BF),
-                pltpu.VMEM((2 * R1, 2 * SLAB), F32),
+                pltpu.VMEM((YB, K1, 2 * SLAB), BF),
                 pltpu.VMEM((2 * R1, K2), BF),
-                pltpu.VMEM((2 * R1, 2 * SLAB), F32),
                 pltpu.VMEM((R1 * 24, 128), F32),
             ],
         ),
@@ -174,7 +182,7 @@
     lane = ky // YB * L + kz
     tile = (ky % YB * L + kx) * 3 + lane // 128
     place = lax.iota(jnp.int32, gvec_index.shape[0])
-    return tile * 128 + (place - lane) % 128
+    return tile * 1024 + (place - lane) % 128
 
 
 def local(valence_store, band_owner, valence_energy, cond_bands, cond_energy, gvec_index):

time: 102 us -> 94.3 us (0.925)
  Pallas kernels: 22.5 us -> 15.4 us
    pallas_call x1, Pallas kernels: 22.5 us -> 15.4 us  [pair_elements(): pl.pallas_call(pairs_kernel, out_shape=jax.ShapeDtypeStruct((rows, 128),...]
  transfers between devices with their start and end apart: 4 -> 4, of which waited for: 3 -> 3; matrix products, arithmetic and copies ran while one was open for 1% -> 2% of each run, Pallas kernels for 0% -> 0%
where the time goes in v1:
time: 94.3 us; the launch traced here: 93.7 us
  blocking collectives  30.9 us (33%)
  waiting for transfers between devices  22.7 us (24%)
  starting transfers between devices  15.5 us (16%)
  Pallas kernels  15.4 us (16%)
  between operations  3.47 us (4%)
  local copies, waits for them, and re-layouts  2.87 us (3%)
  other arithmetic  2.63 us (3%)
    all_to_all x1, blocking collectives, local(): came = lax.all_to_all(sent, 'col', 0, 0, tiled=True)  19.4 us
    pallas_call x1, Pallas kernels, pair_elements(): pl.pallas_call(pairs_kernel, out_shape=jax.ShapeDtypeStruct((rows, 128),...  15.4 us
    all_to_all x1, blocking collectives, local(): summands = lax.all_to_all(part, 'val', 0, 0, tiled=True)  11.5 us
    all_to_all x1, waiting for transfers between devices, local(): lax.all_to_all(half.reshape(chips, 7, 8, 128), 'col', 0, 0, tiled=True, a...  11.1 us
    all_to_all x1, starting transfers between devices, local(): lax.all_to_all(half.reshape(chips, 7, 8, 128), 'col', 0, 0, tiled=True, a...  11 us
    all_to_all x1, waiting for transfers between devices, local(): lax.all_to_all(again, 'col', 0, 0, tiled=True, axis_index_groups=groups)  10.3 us
    all_to_all x1, starting transfers between devices, local(): lax.all_to_all(again, 'col', 0, 0, tiled=True, axis_index_groups=groups)  4.35 us
  transfers between devices with their start and end apart: 4, of which 3 were waited for; matrix products, arithmetic and copies ran while one was open for 2% of the time, Pallas kernels for 0%

profile of v1, /device:TPU:32, one launch (start us, length us, event | category | flops | bytes accessed | tf_op | source)
XLA Modules:
  0.0 93.7 jit_solution(92891052970479147)
XLA Ops:
  0.0 0.0 copy-start.5
  0.0 0.0 copy-start.4
  0.0 0.0 copy-start
  0.0 0.0 copy-start.1
  0.0 0.0 copy-start.2
  0.0 0.0 copy-start.3
  0.0 1.3 %convert_element_type.27 = f16[1,1,2,48,2304]{4,3,2,1,0:T(8,128)(2,1)S(1)} convert(f32[1,1,2,48,2304]{4,3,2,1,0:T(8,128)} %param.10) | non-fusion elementwise | flops 221184 | bytes 1327104 | tf_op jit(solution)/shard_map/convert_element_type | solution.py:196
  1.4 0.1 fusion.4
  1.4 0.1 collective-permute-start
  1.5 1.2 %dynamic_slice.14 = s32[1]{0:T(128)} dynamic-slice(s32[8]{0:T(128)} %param.11, s32[]{:T(128)S(6)} %select_n.89), dynamic_slice_sizes={1} | dynamic-slice | bytes 12 | tf_op jit(solution)/shard_map/dynamic_slice | solution.py:194
  4.7 0.0 collective-permute-done
  4.7 0.8 fusion.3
  5.5 11.0 %all-to-all-start = ((f16[16,7,8,128]{3,2,1,0:T(8,128)(2,1)}), f16[16,7,8,128]{3,2,1,0:T(8,128)(2,1)S(1)}, u32[]{:S(2)}, u32[]{:S(2)}) async-start(f16[16,7,8,128]{3,2,1,0:T(8,128)(2,1)} %bitcast.6), calls=%async_computation | async-start | bytes 458752 | tf_op jit(solution)/shard_map/all_to_all | solution.py:205
  17.2 11.1 %all-to-all-done = f16[16,7,8,128]{3,2,1,0:T(8,128)(2,1)S(1)} async-done(((f16[16,7,8,128]{3,2,1,0:T(8,128)(2,1)}), f16[16,7,8,128]{3,2,1,0:T(8,128)(2,1)S(1)}, u32[]{:S(2)}, u32[]{:S(2)}) %all-to-all-start) | async-done | bytes 229408 | tf_op jit(solution)/shard_map/all_to_all | solution.py:205
  28.3 0.7 broadcast_in_dim.22
  29.0 4.4 %all-to-all-start.1 = ((f16[16,7,8,128]{3,2,1,0:T(8,128)(2,1)}), f16[16,7,8,128]{3,2,1,0:T(8,128)(2,1)S(1)}, u32[]{:S(2)}, u32[]{:S(2)}) async-start(f16[16,7,8,128]{3,2,1,0:T(8,128)(2,1)} %broadcast_in_dim.22), calls=%async_computation.1 | async-start | bytes 458752 | tf_op jit(solution)/shard_map/all_to_all | solution.py:208
  34.0 0.0 copy-done.5
  34.1 10.3 %all-to-all-done.1 = f16[16,7,8,128]{3,2,1,0:T(8,128)(2,1)S(1)} async-done(((f16[16,7,8,128]{3,2,1,0:T(8,128)(2,1)}), f16[16,7,8,128]{3,2,1,0:T(8,128)(2,1)S(1)}, u32[]{:S(2)}, u32[]{:S(2)}) %all-to-all-start.1) | async-done | bytes 229408 | tf_op jit(solution)/shard_map/all_to_all | solution.py:208
  44.3 0.0 collective-permute-start.1
  44.3 0.1 pad_maximum_fusion.2
  44.4 0.0 copy-done.4
  44.4 0.1 fusion.15.word
  44.5 1.3 %collective-permute-done.1 = f16[112,8,128]{2,1,0:T(8,128)(2,1)S(1)} collective-permute-done((f16[112,8,128]{2,1,0:T(8,128)(2,1)S(1)}, f16[112,8,128]{2,1,0:T(8,128)(2,1)S(1)}, u32[]{:S(2)}, u32[]{:S(2)}) %collective-permute-start.1) | collective-permute-done | bytes 229408 | tf_op jit(solution)/shard_map/ppermute | solution.py:209
  45.8 0.1 select_bitcast_fusion.1
  46.0 0.1 pad_maximum_fusion
  46.1 0.1 convert_bitcast_fusion.v_ref
  46.2 0.1 broadcast_in_dim.23.scale_ref
  46.2 0.0 copy-done
  46.2 0.0 copy-done.1
  46.2 0.0 copy-done.2
  46.2 0.0 copy-done.3
  46.2 15.4 %pairs.1 = bf16[256,128]{1,0:T(8,128)(2,1)S(1)} custom-call(s32[4096]{0:T(1024)S(1)} %fusion.15.word, f32[2,48,2304]{2,1,0:T(8,128)S(1)} %convert_bitcast_fusion.v_ref, f32[4,2,48,2304]{3,2,1,0:T(8,128)} %c_ref.1, f32[8,128]{1,0:T(8,128)S(1)} %broadcast_in_dim.23.scale_ref, f32[96,96]{1,0:T(8,128)S(1)} %copy-done.1, f32[2,48,384]{2,1,0:T(8,128)S(1)} %copy-done, ...), custom_call_target="tpu_custom_call" | custom-call | tf_op jit(solution)/shard_map/pairs/pallas_call | solution.py:151
  61.7 19.4 %all_to_all.20 = bf16[32,5,8,128]{3,2,1,0:T(8,128)(2,1)S(1)} all-to-all(bf16[32,5,8,128]{3,2,1,0:T(8,128)(2,1)S(1)} %pad_maximum_fusion.1), channel_id=1, replica_groups=mesh['val'=8,'col'=32] {'col'}, dimensions={0} | all-to-all | bytes 655360 | tf_op jit(solution)/shard_map/all_to_all | solution.py:223
  81.1 0.3 fusion.1
  81.4 11.5 %all_to_all.21 = bf16[8,64,256]{2,1,0:T(8,128)(2,1)S(1)} all-to-all(bf16[8,64,256]{2,1,0:T(8,128)(2,1)S(1)} %bitcast.58), channel_id=1, replica_groups=mesh['val'=8,'col'=32] {'val'}, dimensions={0} | all-to-all | bytes 524288 | tf_op jit(solution)/shard_map/all_to_all | solution.py:232
  93.0 0.6 copy.17
  (11 shorter events, 0.2 us)
Async XLA Ops:
  0.0 34.0 %copy-start.5 = (f32[4]{0:T(128)S(1)}, f32[4]{0:T(128)}, u32[]{:S(2)}) copy-start(f32[4]{0:T(128)} %param.14) | copy-start | bytes 52
  0.0 44.4 %copy-start.4 = (s32[4096]{0:T(1024)S(1)}, s32[4096]{0:T(1024)}, u32[]{:S(2)}) copy-start(s32[4096]{0:T(1024)} %param.15) | copy-start | bytes 49156
  0.0 46.2 %copy-start = (f32[2,48,384]{2,1,0:T(8,128)S(1)}, f32[2,48,384]{2,1,0:T(8,128)}, u32[]{:S(2)}) copy-start(f32[2,48,384]{2,1,0:T(8,128)} %constant.133.clone.t2a) | copy-start | bytes 442372
  0.0 46.2 %copy-start.1 = (f32[96,96]{1,0:T(8,128)S(1)}, f32[96,96]{1,0:T(8,128)}, u32[]{:S(2)}) copy-start(f32[96,96]{1,0:T(8,128)} %constant.132.clone.t1) | copy-start | bytes 110596
  0.0 46.2 %copy-start.2 = (f32[2,8,384]{2,1,0:T(8,128)S(1)}, f32[2,8,384]{2,1,0:T(8,128)}, u32[]{:S(2)}) copy-start(f32[2,8,384]{2,1,0:T(8,128)} %constant.134.clone.t2b) | copy-start | bytes 73732
  0.0 46.2 %copy-start.3 = (f32[2,8,384]{2,1,0:T(8,128)S(1)}, f32[2,8,384]{2,1,0:T(8,128)}, u32[]{:S(2)}) copy-start(f32[2,8,384]{2,1,0:T(8,128)} %constant.135.clone.tw) | copy-start | bytes 73732
  1.4 3.3 %collective-permute-start = (f16[112,8,128]{2,1,0:T(8,128)(2,1)S(1)}, f16[112,8,128]{2,1,0:T(8,128)(2,1)S(1)}, u32[]{:S(2)}, u32[]{:S(2)}) collective-permute-start(f16[112,8,128]{2,1,0:T(8,128)(2,1)S(1)} %fusion.4), channel_id=1, source_target_pairs={{0,1},{1,0},{2,3},{3,2},{4,5},{5,4},{6,7},{7,6},{8,9},{9,8},{10,11... | collective-permute-start | bytes 688136 | tf_op jit(solution)/shard_map/ppermute | solution.py:202
  5.5 22.8 %all-to-all-start = ((f16[16,7,8,128]{3,2,1,0:T(8,128)(2,1)}), f16[16,7,8,128]{3,2,1,0:T(8,128)(2,1)S(1)}, u32[]{:S(2)}, u32[]{:S(2)}) async-start(f16[16,7,8,128]{3,2,1,0:T(8,128)(2,1)} %bitcast.6), calls=%async_computation | async-start | bytes 458752 | tf_op jit(solution)/shard_map/all_to_all | solution.py:205
  29.0 15.3 %all-to-all-start.1 = ((f16[16,7,8,128]{3,2,1,0:T(8,128)(2,1)}), f16[16,7,8,128]{3,2,1,0:T(8,128)(2,1)S(1)}, u32[]{:S(2)}, u32[]{:S(2)}) async-start(f16[16,7,8,128]{3,2,1,0:T(8,128)(2,1)} %broadcast_in_dim.22), calls=%async_computation.1 | async-start | bytes 458752 | tf_op jit(solution)/shard_map/all_to_all | solution.py:208
  44.3 1.5 %collective-permute-start.1 = (f16[112,8,128]{2,1,0:T(8,128)(2,1)S(1)}, f16[112,8,128]{2,1,0:T(8,128)(2,1)S(1)}, u32[]{:S(2)}, u32[]{:S(2)}) collective-permute-start(f16[112,8,128]{2,1,0:T(8,128)(2,1)S(1)} %bitcast.57), channel_id=1, source_target_pairs={{0,1},{1,0},{2,3},{3,2},{4,5},{5,4},{6,7},{7,6},{8,9},{9,8},{10,11... | collective-permute-start | bytes 688136 | tf_op jit(solution)/shard_map/ppermute | solution.py:209

commit v2 on v1

v2 whole, which is shorter than its diff:
```python
import numpy as np

import jax
import jax.numpy as jnp
from jax import lax
from jax.experimental import pallas as pl
from jax.experimental.pallas import tpu as pltpu
from jax.sharding import PartitionSpec as P

ROW_DEV = 64
L = 48
YI = 8
YB = L // YI
SLAB = YI * L
R1 = YB * L
K1 = 6 * L
K2 = 6 * SLAB
ROOT = 0.75 ** 0.5
BF = jnp.bfloat16
F32 = jnp.float32


def tables():
    def trig(phase):
        angle = 2.0 * np.pi * (phase % L) / L
        return np.stack([np.cos(angle), np.sin(angle)]).astype(np.float32)

    r = np.arange(L)
    ka_of = np.repeat(np.arange(YI), L)
    kz_of = np.tile(r, YI)
    t1 = trig(r[:, None] * r[None, :])
    t1 = np.block([[t1[0], t1[1]], [-t1[1], t1[0]]])
    t2a = trig(r[:, None] * kz_of[None, :])
    t2b = trig(6 * np.arange(YI)[:, None] * ka_of[None, :])
    yi_of = np.repeat(np.arange(YI), L)
    tw = trig(np.arange(8)[:, None] * yi_of[None, :])
    return t1, t2a, t2b, tw


def split(value):
    hi = value.astype(BF)
    return hi, (value - hi.astype(F32)).astype(BF)


def dft3(s):
    (r0, i0), (r1, i1), (r2, i2) = s
    tr, ti = r1 + r2, i1 + i2
    ur, ui = r0 - 0.5 * tr, i0 - 0.5 * ti
    dr, di = (r1 - r2) * ROOT, (i1 - i2) * ROOT
    return [(r0 + tr, i0 + ti), (ur + di, ui - dr), (ur - di, ui + dr)]


def dft6(p):
    a = [(p[m][0] + p[m + 3][0], p[m][1] + p[m + 3][1]) for m in range(3)]
    b = [(p[m][0] - p[m + 3][0], p[m][1] - p[m + 3][1]) for m in range(3)]
    b[1] = (p[4][0] - p[1][0], p[4][1] - p[1][1])
    even = dft3(a)
    odd = dft3(b)
    return [even[0], odd[2], even[1], odd[0], even[2], odd[1]]


def fill_tables(t1, t2a, t2b, a1, b2):
    hi, lo = split(t1[...])
    a1[:, 0:2 * L] = hi
    a1[:, 2 * L:4 * L] = lo
    a1[:, 4 * L:6 * L] = hi
    for yi in range(YI):
        cb = t2b[0, yi:yi + 1, :]
        sb = t2b[1, yi:yi + 1, :]
        cos = t2a[0] * cb - t2a[1] * sb
        sin = t2a[1] * cb + t2a[0] * sb
        for value, negative, spots in ((cos, False, ((0, 0), (1, 1))), (sin, True, ((1, 0), (0, 1)))):
            hi, lo = split(value)
            for ri, half in spots:
                flip = negative and ri == 0
                high, low = (-hi, -lo) if flip else (hi, lo)
                cols = slice(half * SLAB, (half + 1) * SLAB)
                r0 = ri * SLAB + yi * L
                b2[r0:r0 + L, cols] = high
                b2[2 * SLAB + r0:2 * SLAB + r0 + L, cols] = low
                b2[4 * SLAB + r0:4 * SLAB + r0 + L, cols] = high


def pairs_kernel(
    word_any, c_any, v_ref, scale_ref, t1, t2a, t2b, tw, hot_ref, out_ref,
    word, c_ref, a1, b2, p3, l2, grid, d0, d1, d2, d3, sems, word_sem,
):
    def fetch(step):
        pair = pl.ds(2 * step, 2)
        return pltpu.make_async_copy(c_any.at[pair], c_ref.at[pair], sems.at[step])

    word_copy = pltpu.make_async_copy(word_any, word, word_sem)
    fetch(0).start()
    fetch(1).start()
    word_copy.start()
    fill_tables(t1, t2a, t2b, a1, b2)

    def bands(step, carry):
        fetch(step).wait()
        for lt in range(SLAB // 128):
            for xc in range(L // 16):
                xs = slice(xc * 16, xc * 16 + 16)
                for bb in range(2):
                    cols = slice(bb * SLAB + lt * 128, bb * SLAB + lt * 128 + 128)
                    p = []
                    for yb in range(YB):
                        lanes = slice(yb * SLAB + lt * 128, yb * SLAB + lt * 128 + 128)
                        v0 = v_ref[0, xs, lanes]
                        v1 = v_ref[1, xs, lanes]
                        c0 = c_ref[2 * step + bb, 0, xs, lanes]
                        c1 = c_ref[2 * step + bb, 1, xs, lanes]
                        p.append((v0 * c0 + v1 * c1, v0 * c1 - v1 * c0))
                    for kb, q in enumerate(dft6(p)):
                        for ri in range(2):
                            hi, lo = split(q[ri])
                            r0 = ri * L + xc * 16
                            p3[kb, r0:r0 + 16, cols] = hi
                            p3[kb, 2 * L + r0:2 * L + r0 + 16, cols] = hi
                            p3[kb, 4 * L + r0:4 * L + r0 + 16, cols] = lo
        for kb in range(YB):
            z = jnp.dot(a1[...], p3[kb], preferred_element_type=F32)
            cw = tw[0, kb:kb + 1, :]
            sw = tw[1, kb:kb + 1, :]
            for bb in range(2):
                zr = z[:L, bb * SLAB:(bb + 1) * SLAB]
                zi = z[L:, bb * SLAB:(bb + 1) * SLAB]
                rows = slice(bb * R1 + kb * L, bb * R1 + kb * L + L)
                for ri, value in enumerate((zr * cw + zi * sw, zi * cw - zr * sw)):
                    hi, lo = split(value)
                    l2[rows, ri * SLAB:(ri + 1) * SLAB] = hi
                    l2[rows, (2 + ri) * SLAB:(3 + ri) * SLAB] = hi
                    l2[rows, (4 + ri) * SLAB:(5 + ri) * SLAB] = lo
        y = jnp.dot(l2[...], b2[...], preferred_element_type=F32)
        for bb in range(2):
            scale = scale_ref[pl.ds(2 * step + bb, 1), :]
            for ri in range(2):
                for t in range(3):
                    c0 = ri * SLAB + t * 128
                    start = t * 8 + ri * 4 + bb + 2 * step
                    grid[pl.ds(start, R1, stride=24), :] = y[bb * R1:(bb + 1) * R1, c0:c0 + 128] * scale
        return carry

    lax.fori_loop(0, 2, bands, 0)

    row = lax.broadcasted_iota(jnp.int32, (16, 8 * 128), 0)
    comp = lax.broadcasted_iota(jnp.int32, (16, 8 * 128), 1) // 128
    pick = [(row == comp + 8 * h).astype(F32).astype(BF) for h in range(2)]

    def copy(p, d, first, last):
        for j in range(first, last):
            h, i = divmod(j, 128)
            start = pl.multiple_of(word[p * 256 + j], 8)
            d[h][pl.ds(i // 8 * 64 + i % 8, 8, stride=8), :] = grid[pl.ds(start, 8), :]

    def partial_sum(p, d, k):
        h, c0 = divmod(2 * k, 8)
        hot = hot_ref[p * 256 + h * 128:p * 256 + h * 128 + 128, :]
        rows = []
        for c in (c0, c0 + 1):
            cell = jnp.concatenate([d[h][ib * 64 + c * 8:ib * 64 + c * 8 + 8, :] for ib in range(16)], 0)
            rows.append(cell.astype(BF) * hot)
        return lax.dot_general(
            pick[h][:, c0 * 128:c0 * 128 + 256], jnp.concatenate(rows, 1),
            (((1,), (1,)), ((), ())), preferred_element_type=F32,
        )

    word_copy.wait()
    buffers = (d0, d1), (d2, d3)
    count = out_ref.shape[0] // 16
    copy(0, buffers[0], 0, 256)
    for p in range(count):
        total = None
        for k in range(8):
            got = partial_sum(p, buffers[p % 2], k)
            total = got if total is None else total + got
            if p + 1 < count:
                copy(p + 1, buffers[(p + 1) % 2], 32 * k, 32 * k + 32)
        out_ref[p * 16:p * 16 + 16, :] = total.astype(BF)


def pair_elements(valence, cond, scale, words, hot):
    count = words.shape[0]
    rows = count // 128 * 8
    t1, t2a, t2b, tw = tables()
    vmem = pl.BlockSpec(memory_space=pltpu.VMEM)
    hbm = pl.BlockSpec(memory_space=pl.ANY)
    return pl.pallas_call(
        pairs_kernel,
        out_shape=jax.ShapeDtypeStruct((rows, 128), BF),
        in_specs=[hbm, hbm] + [vmem] * 7,
        out_specs=vmem,
        scratch_shapes=[
            pltpu.SMEM((count,), jnp.int32),
            pltpu.VMEM(cond.shape, F32),
            pltpu.VMEM((2 * L, K1), BF),
            pltpu.VMEM((K2, 2 * SLAB), BF),
            pltpu.VMEM((YB, K1, 2 * SLAB), BF),
            pltpu.VMEM((2 * R1, K2), BF),
            pltpu.VMEM((R1 * 24, 128), F32),
        ] + [pltpu.VMEM((8 * 128, 128), F32)] * 4 + [
            pltpu.SemaphoreType.DMA((2,)),
            pltpu.SemaphoreType.DMA(()),
        ],
        compiler_params=pltpu.CompilerParams(vmem_limit_bytes=40 << 20),
        name="pairs",
    )(words, cond, valence, scale, t1, t2a, t2b, tw, hot)


def gather_words(gvec_index):
    kx = gvec_index // (L * L)
    ky = gvec_index // L % L
    kz = gvec_index % L
    lane = ky // YB * L + kz
    tile = (ky % YB * L + kx) * 3 + lane // 128
    hot = (lane % 128)[:, None] == lax.iota(jnp.int32, 128)[None, :]
    return tile * 8, hot.astype(F32).astype(BF)


def local(valence_store, band_owner, valence_energy, cond_bands, cond_energy, gvec_index):
    n_col = lax.axis_size("col")
    n_val = lax.axis_size("val")
    chips = n_col // 2
    core = lax.axis_index("col") & 1
    bands = lax.iota(jnp.int32, band_owner.shape[0])
    owner = jnp.sum(jnp.where(bands == lax.axis_index("val"), band_owner, 0))
    spread = jnp.broadcast_to(band_owner[:, None], (band_owner.shape[0], 128))
    owner_core = jnp.sum(jnp.where(bands[:, None] == lax.axis_index("val"), spread, 0), 0) & 1

    tiles = valence_store[0, 0].astype(jnp.float16).reshape(2, 6, 8, 18, 128)
    tiles = tiles.transpose(0, 1, 3, 2, 4).reshape(2, 108, 8, 128)
    tiles = jnp.pad(tiles, ((0, 0), (0, 4), (0, 0), (0, 0)))
    swap = [(i, i ^ 1) for i in range(n_col)]
    mine = lax.dynamic_index_in_dim(tiles, core, 0, False)
    theirs = lax.dynamic_index_in_dim(tiles, 1 - core, 0, False)
    other = lax.ppermute(theirs, "col", swap)
    half = jnp.where(owner_core[None, None, :] == core, mine, other)
    groups = [[q * 2 + c for q in range(chips)] for c in range(2)]
    got = lax.all_to_all(half.reshape(chips, 7, 8, 128), "col", 0, 0, tiled=True, axis_index_groups=groups)
    chunk = lax.dynamic_index_in_dim(got, owner >> 1, 0, True)
    again = jnp.broadcast_to(chunk, (chips, 7, 8, 128))
    half = lax.all_to_all(again, "col", 0, 0, tiled=True, axis_index_groups=groups).reshape(112, 8, 128)
    other = lax.ppermute(half, "col", swap)
    both = jnp.stack([jnp.where(core == 0, half, other), jnp.where(core == 0, other, half)], 0)
    valence = both[:, :108].reshape(2, 6, 18, 8, 128).transpose(0, 1, 3, 2, 4).reshape(2, L, L * L).astype(F32)

    total_bands = cond_bands.shape[0] * n_col * n_val
    constant = total_bands ** (-0.25) * L ** (-1.5)
    scaling = jnp.sqrt(2.0 / (cond_energy - valence_energy[0])) * constant
    scale = jnp.broadcast_to(scaling[:, None], (scaling.shape[0], 128))
    pairs = pair_elements(valence, cond_bands, scale, *gather_words(gvec_index)).reshape(n_col, 8, 128)

    row_count = ROW_DEV * n_val
    row_blocks = row_count // 128
    heads = pairs[:row_blocks]
    by_core = pairs.reshape(chips, 2, 8, 128)
    mine = lax.dynamic_index_in_dim(by_core, core, 1, False)
    theirs = lax.dynamic_index_in_dim(by_core, 1 - core, 1, False)
    other = lax.ppermute(jnp.concatenate([theirs, heads], 0), "col", swap)
    spread = lambda block: jnp.broadcast_to(block[None], (chips, row_blocks, 8, 128))
    sent = jnp.concatenate(
        [mine[:, None], spread(heads), other[:chips, None], spread(other[chips:])], 1
    )
    came = lax.all_to_all(sent, "col", 0, 0, tiled=True, axis_index_groups=groups)
    came = came.reshape(n_col, 1 + row_blocks, 8, 128)
    col = came[:, 0]
    turned = jnp.concatenate([-col[:, 4:], col[:, :4]], 1)
    right = jnp.concatenate([col, turned], 2).reshape(n_col * 8, 256)
    left = came[:, 1:].transpose(1, 0, 2, 3).reshape(row_blocks, n_col * 8, 128)
    part = -lax.dot_general(
        left, right, (((1,), (0,)), ((), ())), preferred_element_type=F32
    )
    part = part.reshape(n_val, ROW_DEV, 256).astype(BF)
    summands = lax.all_to_all(part, "val", 0, 0, tiled=True)
    total = jnp.sum(summands.astype(F32), 0)
    return total.reshape(ROW_DEV, 2, 128).transpose(1, 0, 2)


def solution(mesh):
    return jax.shard_map(
        local,
        mesh=mesh,
        in_specs=(
            P("val", "col", None, None, None),
            P(),
            P("val"),
            P("col", None, None, None),
            P("col"),
            P(),
        ),
        out_specs=P(None, "val", "col"),
        check_vma=False,
    )
```

time: 94.3 us -> 92.9 us (0.985)
  other arithmetic: 2.63 us -> 5.76 us
  blocking collectives: 30.9 us -> 28.7 us
  between operations: 3.47 us -> 1.54 us
  Pallas kernels: 15.4 us -> 13.9 us
    all_to_all x1, blocking collectives: 19.4 us -> 17.1 us  [local(): lax.all_to_all(sent, 'col', 0, 0, tiled=True, axis_index_groups=groups)]
    unnamed x13 -> x17, local copies, waits for them, and re-layouts: 0.04 us -> 2.04 us
    convert_element_type x0 -> x1, other arithmetic: none -> 1.87 us  [gather_words(): return (tile * 8, hot.astype(F32).astype(BF))]
    pallas_call x1, Pallas kernels: 15.4 us -> 13.9 us  [pair_elements(): pl.pallas_call(pairs_kernel, out_shape=jax.ShapeDtypeStruct((rows, 128),...]
    reduce_sum x0 -> x2, other arithmetic: none -> 1.37 us  [the longest x1 0.74 us: local(): jnp.sum(jnp.where(bands[:, None] == lax.axis_index('val'), spread, 0), 0)]
    ppermute x1, waiting for transfers between devices: 1.33 us -> 0.01 us  [local(): other = lax.ppermute(half, 'col', swap)]
    dynamic_slice x1, local copies, waits for them, and re-layouts: 1.24 us -> 0.02 us  [local(): mine = lax.dynamic_index_in_dim(by_core, core, 1, False)]
    all_to_all x1, waiting for transfers between devices: 11.1 us -> 9.96 us  [local(): lax.all_to_all(half.reshape(chips, 7, 8, 128), 'col', 0, 0, tiled=True, a...]
  transfers between devices with their start and end apart: 4 -> 5, of which waited for: 3 -> 4; matrix products, arithmetic and copies ran while one was open for 2% -> 4% of each run, Pallas kernels for 0% -> 0%
where the time goes in v2:
time: 92.9 us; the launch traced here: 92.5 us
  blocking collectives  28.7 us (31%)
  waiting for transfers between devices  22.4 us (24%)
  starting transfers between devices  16.2 us (17%)
  Pallas kernels  13.9 us (15%)
  other arithmetic  5.76 us (6%)
  local copies, waits for them, and re-layouts  3.65 us (4%)
  between operations  1.54 us (2%)
    all_to_all x1, blocking collectives, local(): lax.all_to_all(sent, 'col', 0, 0, tiled=True, axis_index_groups=groups)  17.1 us
    pallas_call x1, Pallas kernels, pair_elements(): pl.pallas_call(pairs_kernel, out_shape=jax.ShapeDtypeStruct((rows, 128),...  13.9 us
    all_to_all x1, blocking collectives, local(): summands = lax.all_to_all(part, 'val', 0, 0, tiled=True)  11.6 us
    all_to_all x1, starting transfers between devices, local(): lax.all_to_all(half.reshape(chips, 7, 8, 128), 'col', 0, 0, tiled=True, a...  11 us
    all_to_all x1, waiting for transfers between devices, local(): lax.all_to_all(again, 'col', 0, 0, tiled=True, axis_index_groups=groups)  10.9 us
    all_to_all x1, waiting for transfers between devices, local(): lax.all_to_all(half.reshape(chips, 7, 8, 128), 'col', 0, 0, tiled=True, a...  9.96 us
    all_to_all x1, starting transfers between devices, local(): lax.all_to_all(again, 'col', 0, 0, tiled=True, axis_index_groups=groups)  4.49 us
    unnamed x17, local copies, waits for them, and re-layouts  2.04 us
  transfers between devices with their start and end apart: 5, of which 4 were waited for; matrix products, arithmetic and copies ran while one was open for 4% of the time, Pallas kernels for 0%

profile of v2, /device:TPU:32, one launch (start us, length us, event | category | flops | bytes accessed | tf_op | source)
XLA Modules:
  0.0 92.5 jit_solution(2878012190510121446)
XLA Ops:
  0.0 0.0 copy-start.6
  0.0 0.0 copy-start.5
  0.0 1.2 %convert_element_type.33 = f16[1,1,2,48,2304]{4,3,2,1,0:T(8,128)(2,1)S(1)} convert(f32[1,1,2,48,2304]{4,3,2,1,0:T(8,128)} %param.10) | non-fusion elementwise | flops 221184 | bytes 1327104 | tf_op jit(solution)/shard_map/convert_element_type | solution.py:229
  1.2 0.0 copy-start.7
  1.3 0.1 fusion.4
  1.3 0.1 collective-permute-start
  1.4 0.7 select_reduce_fusion
  2.2 0.7 collective-permute-done
  2.9 0.8 fusion.3
  3.7 11.0 %all-to-all-start = ((f16[16,7,8,128]{3,2,1,0:T(8,128)(2,1)}), f16[16,7,8,128]{3,2,1,0:T(8,128)(2,1)S(1)}, u32[]{:S(2)}, u32[]{:S(2)}) async-start(f16[16,7,8,128]{3,2,1,0:T(8,128)(2,1)} %bitcast.5), calls=%async_computation | async-start | bytes 458752 | tf_op jit(solution)/shard_map/all_to_all | solution.py:238
  14.7 0.0 copy-done.6
  14.7 0.6 select_reduce_fusion.1
  16.0 10.0 %all-to-all-done = f16[16,7,8,128]{3,2,1,0:T(8,128)(2,1)S(1)} async-done(((f16[16,7,8,128]{3,2,1,0:T(8,128)(2,1)}), f16[16,7,8,128]{3,2,1,0:T(8,128)(2,1)S(1)}, u32[]{:S(2)}, u32[]{:S(2)}) %all-to-all-start) | async-done | bytes 229408 | tf_op jit(solution)/shard_map/all_to_all | solution.py:238
  26.0 0.7 broadcast_in_dim.71
  26.7 4.5 %all-to-all-start.1 = ((f16[16,7,8,128]{3,2,1,0:T(8,128)(2,1)}), f16[16,7,8,128]{3,2,1,0:T(8,128)(2,1)S(1)}, u32[]{:S(2)}, u32[]{:S(2)}) async-start(f16[16,7,8,128]{3,2,1,0:T(8,128)(2,1)} %broadcast_in_dim.71), calls=%async_computation.1 | async-start | bytes 458752 | tf_op jit(solution)/shard_map/all_to_all | solution.py:241
  31.2 0.0 copy-done.5
  31.2 0.1 add_select_fusion
  31.3 10.9 %all-to-all-done.1 = f16[16,7,8,128]{3,2,1,0:T(8,128)(2,1)S(1)} async-done(((f16[16,7,8,128]{3,2,1,0:T(8,128)(2,1)}), f16[16,7,8,128]{3,2,1,0:T(8,128)(2,1)S(1)}, u32[]{:S(2)}, u32[]{:S(2)}) %all-to-all-start.1) | async-done | bytes 229408 | tf_op jit(solution)/shard_map/all_to_all | solution.py:241
  42.1 0.0 collective-permute-start.1
  42.2 0.0 copy-start.1
  42.2 0.0 copy-start.2
  42.2 0.0 copy-start.3
  42.2 0.0 copy-start.4
  42.2 1.9 %convert_convert_fusion.hot_ref = bf16[4096,128]{1,0:T(8,128)(2,1)S(1)} fusion(s32[4096]{0:T(1024)S(1)} %get-tuple-element.11), kind=kLoop, calls=%fused_computation | loop fusion | flops 1572864 | bytes 1064960 | tf_op jit(solution)/shard_map/convert_element_type | solution.py:216
  44.7 0.0 copy-done.7
  44.7 0.0 collective-permute-done.1
  44.7 0.1 select_bitcast_fusion.1
  44.9 0.1 pad_maximum_fusion
  45.0 0.1 convert_bitcast_fusion.v_ref
  45.1 0.1 broadcast_in_dim.72.scale_ref
  45.2 0.0 copy-done.1
  45.2 0.0 copy-done.2
  45.2 0.0 copy-done.3
  45.2 0.0 copy-done.4
  45.2 0.0 copy-start
  45.2 2.0 %copy-done = f32[4,2,48,2304]{3,2,1,0:T(8,128)S(1)} copy-done((f32[4,2,48,2304]{3,2,1,0:T(8,128)S(1)}, f32[4,2,48,2304]{3,2,1,0:T(8,128)}, u32[]{:S(2)}) %copy-start) | copy-done | bytes 3538968
  47.2 13.9 %pairs.1 = bf16[256,128]{1,0:T(8,128)(2,1)S(1)} custom-call(s32[4096]{0:T(1024)S(1)} %get-tuple-element.12.word_any, f32[4,2,48,2304]{3,2,1,0:T(8,128)S(1)} %copy-done, f32[2,48,2304]{2,1,0:T(8,128)S(1)} %convert_bitcast_fusion.v_ref, f32[4,128]{1,0:T(4,128)S(1)} %broadcast_in_dim.72.scale_ref, f32[96,96]{1,0:T(8,128)S(1)} %copy-done.2, ...), custom_call_target="tpu_custom_call" | custom-call | tf_op jit(solution)/shard_map/pairs/pallas_call | solution.py:187
  61.1 0.6 collective-permute-start.2
  61.7 0.9 collective-permute-done.2
  62.7 17.1 %all_to_all.20 = bf16[16,10,8,128]{3,2,1,0:T(8,128)(2,1)S(1)} all-to-all(bf16[16,10,8,128]{3,2,1,0:T(8,128)(2,1)S(1)} %pad_maximum_fusion.1), channel_id=1, replica_groups={{0,2,4,6,8,10,12,14,16,18,20,22,24,26,28,30},{1,3,5,7,9,11,13,15,17,19,..., dimensions={0} | all-to-all | bytes 655360 | tf_op jit(solution)/shard_map/all_to_all | solution.py:263
  79.9 0.3 fusion.1
  80.2 11.6 %all_to_all.21 = bf16[8,64,256]{2,1,0:T(8,128)(2,1)S(1)} all-to-all(bf16[8,64,256]{2,1,0:T(8,128)(2,1)S(1)} %bitcast.62), channel_id=1, replica_groups=mesh['val'=8,'col'=32] {'val'}, dimensions={0} | all-to-all | bytes 524288 | tf_op jit(solution)/shard_map/all_to_all | solution.py:273
  91.8 0.6 copy.16
  (18 shorter events, 0.3 us)
Async XLA Ops:
  0.0 14.7 %copy-start.6 = (s32[8]{0:T(128)S(1)}, s32[8]{0:T(128)}, u32[]{:S(2)}) copy-start(s32[8]{0:T(128)} %param.11) | copy-start | bytes 100
  0.0 31.2 %copy-start.5 = (s32[4096]{0:T(1024)S(1)}, s32[4096]{0:T(1024)}, u32[]{:S(2)}) copy-start(s32[4096]{0:T(1024)} %param.15) | copy-start | bytes 49156
  1.2 43.5 %copy-start.7 = (f32[4]{0:T(128)S(1)}, f32[4]{0:T(128)}, u32[]{:S(2)}) copy-start(f32[4]{0:T(128)} %param.14) | copy-start | bytes 52
  1.3 1.6 %collective-permute-start = (f16[112,8,128]{2,1,0:T(8,128)(2,1)S(1)}, f16[112,8,128]{2,1,0:T(8,128)(2,1)S(1)}, u32[]{:S(2)}, u32[]{:S(2)}) collective-permute-start(f16[112,8,128]{2,1,0:T(8,128)(2,1)S(1)} %fusion.4), channel_id=1, source_target_pairs={{0,1},{1,0},{2,3},{3,2},{4,5},{5,4},{6,7},{7,6},{8,9},{9,8},{10,11... | collective-permute-start | bytes 688136 | tf_op jit(solution)/shard_map/ppermute | solution.py:235
  3.7 22.3 %all-to-all-start = ((f16[16,7,8,128]{3,2,1,0:T(8,128)(2,1)}), f16[16,7,8,128]{3,2,1,0:T(8,128)(2,1)S(1)}, u32[]{:S(2)}, u32[]{:S(2)}) async-start(f16[16,7,8,128]{3,2,1,0:T(8,128)(2,1)} %bitcast.5), calls=%async_computation | async-start | bytes 458752 | tf_op jit(solution)/shard_map/all_to_all | solution.py:238
  26.7 15.5 %all-to-all-start.1 = ((f16[16,7,8,128]{3,2,1,0:T(8,128)(2,1)}), f16[16,7,8,128]{3,2,1,0:T(8,128)(2,1)S(1)}, u32[]{:S(2)}, u32[]{:S(2)}) async-start(f16[16,7,8,128]{3,2,1,0:T(8,128)(2,1)} %broadcast_in_dim.71), calls=%async_computation.1 | async-start | bytes 458752 | tf_op jit(solution)/shard_map/all_to_all | solution.py:241
  42.1 2.6 %collective-permute-start.1 = (f16[112,8,128]{2,1,0:T(8,128)(2,1)S(1)}, f16[112,8,128]{2,1,0:T(8,128)(2,1)S(1)}, u32[]{:S(2)}, u32[]{:S(2)}) collective-permute-start(f16[112,8,128]{2,1,0:T(8,128)(2,1)S(1)} %bitcast.61), channel_id=1, source_target_pairs={{0,1},{1,0},{2,3},{3,2},{4,5},{5,4},{6,7},{7,6},{8,9},{9,8},{10,11... | collective-permute-start | bytes 688136 | tf_op jit(solution)/shard_map/ppermute | solution.py:242
  42.2 3.0 %copy-start.1 = (f32[2,48,384]{2,1,0:T(8,128)S(1)}, f32[2,48,384]{2,1,0:T(8,128)}, u32[]{:S(2)}) copy-start(f32[2,48,384]{2,1,0:T(8,128)} %constant.114.clone.t2a) | copy-start | bytes 442372
  42.2 3.0 %copy-start.2 = (f32[96,96]{1,0:T(8,128)S(1)}, f32[96,96]{1,0:T(8,128)}, u32[]{:S(2)}) copy-start(f32[96,96]{1,0:T(8,128)} %constant.113.clone.t1) | copy-start | bytes 110596
  42.2 3.0 %copy-start.3 = (f32[2,8,384]{2,1,0:T(8,128)S(1)}, f32[2,8,384]{2,1,0:T(8,128)}, u32[]{:S(2)}) copy-start(f32[2,8,384]{2,1,0:T(8,128)} %constant.116.clone.tw) | copy-start | bytes 73732
  42.2 3.0 %copy-start.4 = (f32[2,8,384]{2,1,0:T(8,128)S(1)}, f32[2,8,384]{2,1,0:T(8,128)}, u32[]{:S(2)}) copy-start(f32[2,8,384]{2,1,0:T(8,128)} %constant.115.clone.t2b) | copy-start | bytes 73732
  45.2 2.0 %copy-start = (f32[4,2,48,2304]{3,2,1,0:T(8,128)S(1)}, f32[4,2,48,2304]{3,2,1,0:T(8,128)}, u32[]{:S(2)}) copy-start(f32[4,2,48,2304]{3,2,1,0:T(8,128)} %c_any.1) | copy-start | bytes 10616836
  61.1 1.5 %collective-permute-start.2 = (bf16[20,8,128]{2,1,0:T(8,128)(2,1)S(1)}, bf16[20,8,128]{2,1,0:T(8,128)(2,1)S(1)}, u32[]{:S(2)}, u32[]{:S(2)}) collective-permute-start(bf16[20,8,128]{2,1,0:T(8,128)(2,1)S(1)} %pad_maximum_fusion.2), channel_id=1, source_target_pairs={{0,1},{1,0},{2,3},{3,2},{4,5},{5,4},{6,7},{7,6},{8,9},{9,8},{10,11... | collective-permute-start | bytes 122888 | tf_op jit(solution)/shard_map/ppermute | solution.py:258

commit v3 on v2

--- a/solution.py
+++ b/solution.py
@@ -59,7 +59,7 @@
     return [even[0], odd[2], even[1], odd[0], even[2], odd[1]]
 
 
-def fill_tables(t1, t2a, t2b, a1, b2):
+def table_kernel(t1, t2a, t2b, a1, b2):
     hi, lo = split(t1[...])
     a1[:, 0:2 * L] = hi
     a1[:, 2 * L:4 * L] = lo
@@ -82,18 +82,19 @@
 
 
 def pairs_kernel(
-    word_any, c_any, v_ref, scale_ref, t1, t2a, t2b, tw, hot_ref, out_ref,
-    word, c_ref, a1, b2, p3, l2, grid, d0, d1, d2, d3, sems, word_sem,
+    word_any, c_any, b2_any, v_ref, scale_ref, tw, a1, hot_ref, out_ref,
+    word, c_ref, b2, p3, l2, grid, d0, d1, d2, d3, sems, word_sem, b2_sem,
 ):
     def fetch(step):
         pair = pl.ds(2 * step, 2)
         return pltpu.make_async_copy(c_any.at[pair], c_ref.at[pair], sems.at[step])
 
     word_copy = pltpu.make_async_copy(word_any, word, word_sem)
+    b2_copy = pltpu.make_async_copy(b2_any, b2, b2_sem)
     fetch(0).start()
+    b2_copy.start()
     fetch(1).start()
     word_copy.start()
-    fill_tables(t1, t2a, t2b, a1, b2)
 
     def bands(step, carry):
         fetch(step).wait()
@@ -130,6 +131,10 @@
                     l2[rows, ri * SLAB:(ri + 1) * SLAB] = hi
                     l2[rows, (2 + ri) * SLAB:(3 + ri) * SLAB] = hi
                     l2[rows, (4 + ri) * SLAB:(5 + ri) * SLAB] = lo
+        @pl.when(step == 0)
+        def _():
+            b2_copy.wait()
+
         y = jnp.dot(l2[...], b2[...], preferred_element_type=F32)
         for bb in range(2):
             scale = scale_ref[pl.ds(2 * step + bb, 1), :]
@@ -178,21 +183,36 @@
         out_ref[p * 16:p * 16 + 16, :] = total.astype(BF)
 
 
-def pair_elements(valence, cond, scale, words, hot):
+def dft_tables():
+    t1, t2a, t2b, tw = tables()
+    vmem = pl.BlockSpec(memory_space=pltpu.VMEM)
+    a1, b2 = pl.pallas_call(
+        table_kernel,
+        out_shape=(
+            jax.ShapeDtypeStruct((2 * L, K1), BF),
+            jax.ShapeDtypeStruct((K2, 2 * SLAB), BF),
+        ),
+        in_specs=[vmem] * 3,
+        out_specs=(vmem, vmem),
+        name="dft_tables",
+    )(t1, t2a, t2b)
+    return a1, b2, jnp.asarray(tw)
+
+
+def pair_elements(valence, cond, scale, words, hot, a1, b2, tw):
     count = words.shape[0]
     rows = count // 128 * 8
-    t1, t2a, t2b, tw = tables()
     vmem = pl.BlockSpec(memory_space=pltpu.VMEM)
-    hbm = pl.BlockSpec(memory_space=pl.ANY)
+    hbm = pl.BlockSpec(memory_space=pltpu.HBM)
+    keep = lambda x: pltpu.with_memory_space_constraint(x, pltpu.HBM)
     return pl.pallas_call(
         pairs_kernel,
         out_shape=jax.ShapeDtypeStruct((rows, 128), BF),
-        in_specs=[hbm, hbm] + [vmem] * 7,
+        in_specs=[hbm, hbm, hbm] + [vmem] * 5,
         out_specs=vmem,
         scratch_shapes=[
             pltpu.SMEM((count,), jnp.int32),
             pltpu.VMEM(cond.shape, F32),
-            pltpu.VMEM((2 * L, K1), BF),
             pltpu.VMEM((K2, 2 * SLAB), BF),
             pltpu.VMEM((YB, K1, 2 * SLAB), BF),
             pltpu.VMEM((2 * R1, K2), BF),
@@ -200,10 +220,11 @@
         ] + [pltpu.VMEM((8 * 128, 128), F32)] * 4 + [
             pltpu.SemaphoreType.DMA((2,)),
             pltpu.SemaphoreType.DMA(()),
+            pltpu.SemaphoreType.DMA(()),
         ],
         compiler_params=pltpu.CompilerParams(vmem_limit_bytes=40 << 20),
         name="pairs",
-    )(words, cond, valence, scale, t1, t2a, t2b, tw, hot)
+    )(words, keep(cond), keep(b2), valence, scale, tw, a1, hot)
 
 
 def gather_words(gvec_index):
@@ -236,18 +257,20 @@
     half = jnp.where(owner_core[None, None, :] == core, mine, other)
     groups = [[q * 2 + c for q in range(chips)] for c in range(2)]
     got = lax.all_to_all(half.reshape(chips, 7, 8, 128), "col", 0, 0, tiled=True, axis_index_groups=groups)
+    total_bands = cond_bands.shape[0] * n_col * n_val
+    constant = total_bands ** (-0.25) * L ** (-1.5)
+    scaling = jnp.sqrt(2.0 / (cond_energy - valence_energy[0])) * constant
+    scale = jnp.broadcast_to(scaling[:, None], (scaling.shape[0], 128))
+    words, hot = gather_words(gvec_index)
     chunk = lax.dynamic_index_in_dim(got, owner >> 1, 0, True)
+    chunk, scale, words, hot, tabs = lax.optimization_barrier((chunk, scale, words, hot, dft_tables()))
     again = jnp.broadcast_to(chunk, (chips, 7, 8, 128))
     half = lax.all_to_all(again, "col", 0, 0, tiled=True, axis_index_groups=groups).reshape(112, 8, 128)
     other = lax.ppermute(half, "col", swap)
     both = jnp.stack([jnp.where(core == 0, half, other), jnp.where(core == 0, other, half)], 0)
     valence = both[:, :108].reshape(2, 6, 18, 8, 128).transpose(0, 1, 3, 2, 4).reshape(2, L, L * L).astype(F32)
 
-    total_bands = cond_bands.shape[0] * n_col * n_val
-    constant = total_bands ** (-0.25) * L ** (-1.5)
-    scaling = jnp.sqrt(2.0 / (cond_energy - valence_energy[0])) * constant
-    scale = jnp.broadcast_to(scaling[:, None], (scaling.shape[0], 128))
-    pairs = pair_elements(valence, cond_bands, scale, *gather_words(gvec_index)).reshape(n_col, 8, 128)
+    pairs = pair_elements(valence, cond_bands, scale, words, hot, *tabs).reshape(n_col, 8, 128)
 
     row_count = ROW_DEV * n_val
     row_blocks = row_count // 128

time: 92.9 us -> 91 us (0.980)
  blocking collectives: 28.7 us -> 44.7 us
  waiting for transfers between devices: 22.4 us -> 7.3 us
  starting transfers between devices: 16.2 us -> 11.4 us
  Pallas kernels: 13.9 us -> 17.9 us
  local copies, waits for them, and re-layouts: 3.65 us -> 0.95 us
    all_to_all x0 -> x1, blocking collectives: none -> 15.7 us  [local(): lax.all_to_all(again, 'col', 0, 0, tiled=True, axis_index_groups=groups)]
    all_to_all x1 -> x0, waiting for transfers between devices: 10.9 us -> none  [local(): lax.all_to_all(again, 'col', 0, 0, tiled=True, axis_index_groups=groups)]
    all_to_all x1, waiting for transfers between devices: 9.96 us -> 4.73 us  [local(): lax.all_to_all(half.reshape(chips, 7, 8, 128), 'col', 0, 0, tiled=True, a...]
    all_to_all x1 -> x0, starting transfers between devices: 4.49 us -> none  [local(): lax.all_to_all(again, 'col', 0, 0, tiled=True, axis_index_groups=groups)]
    pallas_call x0 -> x1, Pallas kernels: none -> 3.17 us  [dft_tables(): pl.pallas_call(table_kernel, out_shape=(jax.ShapeDtypeStruct((2 * L, K1),...]
    unnamed x17 -> x9, local copies, waits for them, and re-layouts: 2.04 us -> 0.03 us
    ppermute x1, waiting for transfers between devices: 0.01 us -> 1.49 us  [local(): other = lax.ppermute(half, 'col', swap)]
  transfers between devices with their start and end apart: 5 -> 4, of which waited for: 4 -> 3; matrix products, arithmetic and copies ran while one was open for 4% -> 4% of each run, Pallas kernels for 0% -> 3%
where the time goes in v3:
time: 91 us; the launch traced here: 90.5 us
  blocking collectives  44.7 us (49%)
  Pallas kernels  17.9 us (20%)
  starting transfers between devices  11.4 us (13%)
  waiting for transfers between devices  7.3 us (8%)
  other arithmetic  6.5 us (7%)
  between operations  1.52 us (2%)
  local copies, waits for them, and re-layouts  0.95 us (1%)
    all_to_all x1, blocking collectives, local(): lax.all_to_all(sent, 'col', 0, 0, tiled=True, axis_index_groups=groups)  17.4 us
    all_to_all x1, blocking collectives, local(): lax.all_to_all(again, 'col', 0, 0, tiled=True, axis_index_groups=groups)  15.7 us
    pallas_call x1, Pallas kernels, pair_elements(): pl.pallas_call(pairs_kernel, out_shape=jax.ShapeDtypeStruct((rows, 128),...  14.7 us
    all_to_all x1, blocking collectives, local(): summands = lax.all_to_all(part, 'val', 0, 0, tiled=True)  11.5 us
    all_to_all x1, starting transfers between devices, local(): lax.all_to_all(half.reshape(chips, 7, 8, 128), 'col', 0, 0, tiled=True, a...  11 us
    all_to_all x1, waiting for transfers between devices, local(): lax.all_to_all(half.reshape(chips, 7, 8, 128), 'col', 0, 0, tiled=True, a...  4.73 us
    pallas_call x1, Pallas kernels, dft_tables(): pl.pallas_call(table_kernel, out_shape=(jax.ShapeDtypeStruct((2 * L, K1),...  3.17 us
    convert_element_type x1, other arithmetic, gather_words(): return (tile * 8, hot.astype(F32).astype(BF))  1.84 us
  transfers between devices with their start and end apart: 4, of which 3 were waited for; matrix products, arithmetic and copies ran while one was open for 4% of the time, Pallas kernels for 3%

profile of v3, /device:TPU:32, one launch (start us, length us, event | category | flops | bytes accessed | tf_op | source)
XLA Modules:
  0.0 90.5 jit_solution(2191956532889750885)
XLA Ops:
  0.0 0.0 copy-start.2
  0.0 0.0 copy-start.3
  0.0 1.2 %convert_element_type.33 = f16[1,1,2,48,2304]{4,3,2,1,0:T(8,128)(2,1)S(1)} convert(f32[1,1,2,48,2304]{4,3,2,1,0:T(8,128)} %param.10) | non-fusion elementwise | flops 221184 | bytes 1327104 | tf_op jit(solution)/shard_map/convert_element_type | solution.py:250
  1.2 0.1 fusion.4
  1.3 0.1 collective-permute-start
  1.4 0.7 select_reduce_fusion
  2.2 0.8 add_select_fusion
  3.0 0.0 collective-permute-done
  3.0 0.8 fusion.3
  3.8 11.0 %all-to-all-start = ((f16[16,7,8,128]{3,2,1,0:T(8,128)(2,1)}), f16[16,7,8,128]{3,2,1,0:T(8,128)(2,1)S(1)}, u32[]{:S(2)}, u32[]{:S(2)}) async-start(f16[16,7,8,128]{3,2,1,0:T(8,128)(2,1)} %bitcast.5), calls=%async_computation | async-start | bytes 458752 | tf_op jit(solution)/shard_map/all_to_all | solution.py:259
  14.8 1.8 %convert_convert_fusion.hot_ref = bf16[4096,128]{1,0:T(8,128)(2,1)S(1)} fusion(s32[4096]{0:T(1024)S(1)} %get-tuple-element.29), kind=kLoop, calls=%fused_computation | loop fusion | flops 1572864 | bytes 1064960 | tf_op jit(solution)/shard_map/convert_element_type | solution.py:237
  16.7 0.0 copy-start.1
  17.3 0.0 copy-done.2
  17.3 0.6 select_reduce_fusion.1
  18.6 3.2 %dft_tables.1 = (bf16[96,288]{1,0:T(8,128)(2,1)}, bf16[2304,768]{1,0:T(8,128)(2,1)}) custom-call(f32[96,96]{1,0:T(8,128)} %constant.113.clone.t1, f32[2,48,384]{2,1,0:T(8,128)} %constant.114.clone.t2a, f32[2,8,384]{2,1,0:T(8,128)} %constant.115.clone.t2b), custom_call_target="tpu_custom_call" | custom-call | tf_op jit(solution)/shard_map/dft_tables/pallas_call | solution.py:189
  21.8 0.0 copy-start
  21.8 0.0 copy-done.3
  21.8 4.7 %all-to-all-done = f16[16,7,8,128]{3,2,1,0:T(8,128)(2,1)S(1)} async-done(((f16[16,7,8,128]{3,2,1,0:T(8,128)(2,1)}), f16[16,7,8,128]{3,2,1,0:T(8,128)(2,1)S(1)}, u32[]{:S(2)}, u32[]{:S(2)}) %all-to-all-start) | async-done | bytes 229408 | tf_op jit(solution)/shard_map/all_to_all | solution.py:259
  26.6 0.1 broadcast_in_dim.70.scale_ref
  26.7 15.7 %all_to_all.20 = f16[16,7,8,128]{3,2,1,0:T(8,128)(2,1)S(1)} all-to-all(f16[16,7,8,128]{3,2,1,0:T(8,128)(2,1)S(1)} %broadcast_in_dim.72), channel_id=1, replica_groups={{0,2,4,6,8,10,12,14,16,18,20,22,24,26,28,30},{1,3,5,7,9,11,13,15,17,19,..., dimensions={0} | all-to-all | bytes 458752 | tf_op jit(solution)/shard_map/all_to_all | solution.py:268
  42.4 0.0 collective-permute-start.1
  42.4 1.5 %collective-permute-done.1 = f16[112,8,128]{2,1,0:T(8,128)(2,1)S(1)} collective-permute-done((f16[112,8,128]{2,1,0:T(8,128)(2,1)S(1)}, f16[112,8,128]{2,1,0:T(8,128)(2,1)S(1)}, u32[]{:S(2)}, u32[]{:S(2)}) %collective-permute-start.1) | collective-permute-done | bytes 229408 | tf_op jit(solution)/shard_map/ppermute | solution.py:269
  43.9 0.2 select_bitcast_fusion.1
  44.1 0.1 pad_maximum_fusion
  44.2 0.1 convert_bitcast_fusion.v_ref
  44.3 0.0 copy-done.1
  44.3 0.0 copy-done
  44.3 14.7 %pairs.1 = bf16[256,128]{1,0:T(8,128)(2,1)S(1)} custom-call(s32[4096]{0:T(1024)S(1)} %get-tuple-element.16.word_any, f32[4,2,48,2304]{3,2,1,0:T(8,128)} %c_any.1, bf16[2304,768]{1,0:T(8,128)(2,1)} %get-tuple-element.17.b2_any, f32[2,48,2304]{2,1,0:T(8,128)S(1)} %convert_bitcast_fusion.v_ref, f32[4,128]{1,0:T(4,128)S(1)} %broadcast_in_dim.70.scale_ref, ...), custom_call_target="tpu_custom_call" | custom-call | tf_op jit(solution)/shard_map/pairs/pallas_call | solution.py:208
  59.1 0.2 collective-permute-start.2
  59.3 1.1 %collective-permute-done.2 = bf16[20,8,128]{2,1,0:T(8,128)(2,1)S(1)} collective-permute-done((bf16[20,8,128]{2,1,0:T(8,128)(2,1)S(1)}, bf16[20,8,128]{2,1,0:T(8,128)(2,1)S(1)}, u32[]{:S(2)}, u32[]{:S(2)}) %collective-permute-start.2) | collective-permute-done | bytes 40992 | tf_op jit(solution)/shard_map/ppermute | solution.py:281
  60.5 17.4 %all_to_all.21 = bf16[16,10,8,128]{3,2,1,0:T(8,128)(2,1)S(1)} all-to-all(bf16[16,10,8,128]{3,2,1,0:T(8,128)(2,1)S(1)} %pad_maximum_fusion.1), channel_id=1, replica_groups={{0,2,4,6,8,10,12,14,16,18,20,22,24,26,28,30},{1,3,5,7,9,11,13,15,17,19,..., dimensions={0} | all-to-all | bytes 655360 | tf_op jit(solution)/shard_map/all_to_all | solution.py:286
  78.0 0.3 fusion.1
  78.3 11.5 %all_to_all.22 = bf16[8,64,256]{2,1,0:T(8,128)(2,1)S(1)} all-to-all(bf16[8,64,256]{2,1,0:T(8,128)(2,1)S(1)} %bitcast.61), channel_id=1, replica_groups=mesh['val'=8,'col'=32] {'val'}, dimensions={0} | all-to-all | bytes 524288 | tf_op jit(solution)/shard_map/all_to_all | solution.py:296
  89.9 0.6 copy.16
  (19 shorter events, 0.3 us)
Async XLA Ops:
  0.0 17.3 %copy-start.2 = (s32[8]{0:T(128)S(1)}, s32[8]{0:T(128)}, u32[]{:S(2)}) copy-start(s32[8]{0:T(128)} %param.11) | copy-start | bytes 100
  0.0 21.8 %copy-start.3 = (f32[4]{0:T(128)S(1)}, f32[4]{0:T(128)}, u32[]{:S(2)}) copy-start(f32[4]{0:T(128)} %param.14) | copy-start | bytes 52
  1.3 1.7 %collective-permute-start = (f16[112,8,128]{2,1,0:T(8,128)(2,1)S(1)}, f16[112,8,128]{2,1,0:T(8,128)(2,1)S(1)}, u32[]{:S(2)}, u32[]{:S(2)}) collective-permute-start(f16[112,8,128]{2,1,0:T(8,128)(2,1)S(1)} %fusion.4), channel_id=1, source_target_pairs={{0,1},{1,0},{2,3},{3,2},{4,5},{5,4},{6,7},{7,6},{8,9},{9,8},{10,11... | collective-permute-start | bytes 688136 | tf_op jit(solution)/shard_map/ppermute | solution.py:256
  3.8 22.8 %all-to-all-start = ((f16[16,7,8,128]{3,2,1,0:T(8,128)(2,1)}), f16[16,7,8,128]{3,2,1,0:T(8,128)(2,1)S(1)}, u32[]{:S(2)}, u32[]{:S(2)}) async-start(f16[16,7,8,128]{3,2,1,0:T(8,128)(2,1)} %bitcast.5), calls=%async_computation | async-start | bytes 458752 | tf_op jit(solution)/shard_map/all_to_all | solution.py:259
  16.7 27.6 %copy-start.1 = (f32[2,8,384]{2,1,0:T(8,128)S(1)}, f32[2,8,384]{2,1,0:T(8,128)}, u32[]{:S(2)}) copy-start(f32[2,8,384]{2,1,0:T(8,128)} %constant.116.clone.tw) | copy-start | bytes 73732
  21.8 22.5 %copy-start = (bf16[96,288]{1,0:T(8,128)(2,1)S(1)}, bf16[96,288]{1,0:T(8,128)(2,1)}, u32[]{:S(2)}) copy-start(bf16[96,288]{1,0:T(8,128)(2,1)} %get-tuple-element.21.a1) | copy-start | bytes 165892
  42.4 1.5 %collective-permute-start.1 = (f16[112,8,128]{2,1,0:T(8,128)(2,1)S(1)}, f16[112,8,128]{2,1,0:T(8,128)(2,1)S(1)}, u32[]{:S(2)}, u32[]{:S(2)}) collective-permute-start(f16[112,8,128]{2,1,0:T(8,128)(2,1)S(1)} %bitcast.60), channel_id=1, source_target_pairs={{0,1},{1,0},{2,3},{3,2},{4,5},{5,4},{6,7},{7,6},{8,9},{9,8},{10,11... | collective-permute-start | bytes 688136 | tf_op jit(solution)/shard_map/ppermute | solution.py:269
  59.1 1.3 %collective-permute-start.2 = (bf16[20,8,128]{2,1,0:T(8,128)(2,1)S(1)}, bf16[20,8,128]{2,1,0:T(8,128)(2,1)S(1)}, u32[]{:S(2)}, u32[]{:S(2)}) collective-permute-start(bf16[20,8,128]{2,1,0:T(8,128)(2,1)S(1)} %pad_maximum_fusion.2), channel_id=1, source_target_pairs={{0,1},{1,0},{2,3},{3,2},{4,5},{5,4},{6,7},{7,6},{8,9},{9,8},{10,11... | collective-permute-start | bytes 122888 | tf_op jit(solution)/shard_map/ppermute | solution.py:281

commit v4 on v2

--- a/solution.py
+++ b/solution.py
@@ -85,22 +85,21 @@
     word_any, c_any, v_ref, scale_ref, t1, t2a, t2b, tw, hot_ref, out_ref,
     word, c_ref, a1, b2, p3, l2, grid, d0, d1, d2, d3, sems, word_sem,
 ):
-    def fetch(step):
-        pair = pl.ds(2 * step, 2)
-        return pltpu.make_async_copy(c_any.at[pair], c_ref.at[pair], sems.at[step])
+    def fetch(band):
+        return pltpu.make_async_copy(c_any.at[band], c_ref.at[band], sems.at[band])
 
     word_copy = pltpu.make_async_copy(word_any, word, word_sem)
-    fetch(0).start()
-    fetch(1).start()
+    for band in range(c_any.shape[0]):
+        fetch(band).start()
     word_copy.start()
     fill_tables(t1, t2a, t2b, a1, b2)
 
     def bands(step, carry):
-        fetch(step).wait()
-        for lt in range(SLAB // 128):
-            for xc in range(L // 16):
-                xs = slice(xc * 16, xc * 16 + 16)
-                for bb in range(2):
+        for bb in range(2):
+            fetch(2 * step + bb).wait()
+            for lt in range(SLAB // 128):
+                for xc in range(L // 16):
+                    xs = slice(xc * 16, xc * 16 + 16)
                     cols = slice(bb * SLAB + lt * 128, bb * SLAB + lt * 128 + 128)
                     p = []
                     for yb in range(YB):
@@ -181,9 +180,9 @@
 def pair_elements(valence, cond, scale, words, hot):
     count = words.shape[0]
     rows = count // 128 * 8
-    t1, t2a, t2b, tw = tables()
     vmem = pl.BlockSpec(memory_space=pltpu.VMEM)
-    hbm = pl.BlockSpec(memory_space=pl.ANY)
+    hbm = pl.BlockSpec(memory_space=pltpu.HBM)
+    cond = pltpu.with_memory_space_constraint(cond, pltpu.HBM)
     return pl.pallas_call(
         pairs_kernel,
         out_shape=jax.ShapeDtypeStruct((rows, 128), BF),
@@ -198,12 +197,12 @@
             pltpu.VMEM((2 * R1, K2), BF),
             pltpu.VMEM((R1 * 24, 128), F32),
         ] + [pltpu.VMEM((8 * 128, 128), F32)] * 4 + [
-            pltpu.SemaphoreType.DMA((2,)),
+            pltpu.SemaphoreType.DMA((cond.shape[0],)),
             pltpu.SemaphoreType.DMA(()),
         ],
         compiler_params=pltpu.CompilerParams(vmem_limit_bytes=40 << 20),
         name="pairs",
-    )(words, cond, valence, scale, t1, t2a, t2b, tw, hot)
+    )(words, cond, valence, scale, *tables(), hot)
 
 
 def gather_words(gvec_index):
@@ -236,18 +235,20 @@
     half = jnp.where(owner_core[None, None, :] == core, mine, other)
     groups = [[q * 2 + c for q in range(chips)] for c in range(2)]
     got = lax.all_to_all(half.reshape(chips, 7, 8, 128), "col", 0, 0, tiled=True, axis_index_groups=groups)
+    total_bands = cond_bands.shape[0] * n_col * n_val
+    constant = total_bands ** (-0.25) * L ** (-1.5)
+    scaling = jnp.sqrt(2.0 / (cond_energy - valence_energy[0])) * constant
+    scale = jnp.broadcast_to(scaling[:, None], (scaling.shape[0], 128))
+    words, hot = gather_words(gvec_index)
     chunk = lax.dynamic_index_in_dim(got, owner >> 1, 0, True)
+    chunk, scale, words, hot = lax.optimization_barrier((chunk, scale, words, hot))
     again = jnp.broadcast_to(chunk, (chips, 7, 8, 128))
     half = lax.all_to_all(again, "col", 0, 0, tiled=True, axis_index_groups=groups).reshape(112, 8, 128)
     other = lax.ppermute(half, "col", swap)
     both = jnp.stack([jnp.where(core == 0, half, other), jnp.where(core == 0, other, half)], 0)
     valence = both[:, :108].reshape(2, 6, 18, 8, 128).transpose(0, 1, 3, 2, 4).reshape(2, L, L * L).astype(F32)
 
-    total_bands = cond_bands.shape[0] * n_col * n_val
-    constant = total_bands ** (-0.25) * L ** (-1.5)
-    scaling = jnp.sqrt(2.0 / (cond_energy - valence_energy[0])) * constant
-    scale = jnp.broadcast_to(scaling[:, None], (scaling.shape[0], 128))
-    pairs = pair_elements(valence, cond_bands, scale, *gather_words(gvec_index)).reshape(n_col, 8, 128)
+    pairs = pair_elements(valence, cond_bands, scale, words, hot).reshape(n_col, 8, 128)
 
     row_count = ROW_DEV * n_val
     row_blocks = row_count // 128

time: 92.9 us -> 88.8 us (0.956)
  blocking collectives: 28.7 us -> 43.9 us
  waiting for transfers between devices: 22.4 us -> 10.4 us
  starting transfers between devices: 16.2 us -> 11.4 us
  local copies, waits for them, and re-layouts: 3.65 us -> 0.97 us
    all_to_all x0 -> x1, blocking collectives: none -> 15.1 us  [local(): lax.all_to_all(again, 'col', 0, 0, tiled=True, axis_index_groups=groups)]
    all_to_all x1 -> x0, waiting for transfers between devices: 10.9 us -> none  [local(): lax.all_to_all(again, 'col', 0, 0, tiled=True, axis_index_groups=groups)]
    all_to_all x1 -> x0, starting transfers between devices: 4.49 us -> none  [local(): lax.all_to_all(again, 'col', 0, 0, tiled=True, axis_index_groups=groups)]
    all_to_all x1, waiting for transfers between devices: 9.96 us -> 7.8 us  [local(): lax.all_to_all(half.reshape(chips, 7, 8, 128), 'col', 0, 0, tiled=True, a...]
    unnamed x17 -> x13, local copies, waits for them, and re-layouts: 2.04 us -> 0.05 us
    ppermute x1, waiting for transfers between devices: 0.01 us -> 1.49 us  [local(): other = lax.ppermute(half, 'col', swap)]
  transfers between devices with their start and end apart: 5 -> 4, of which waited for: 4 -> 3; matrix products, arithmetic and copies ran while one was open for 4% -> 5% of each run, Pallas kernels for 0% -> 0%
where the time goes in v4:
time: 88.8 us; the launch traced here: 88.3 us
  blocking collectives  43.9 us (49%)
  Pallas kernels  13.3 us (15%)
  starting transfers between devices  11.4 us (13%)
  waiting for transfers between devices  10.4 us (12%)
  other arithmetic  6.49 us (7%)
  between operations  1.62 us (2%)
  local copies, waits for them, and re-layouts  0.97 us (1%)
    all_to_all x1, blocking collectives, local(): lax.all_to_all(sent, 'col', 0, 0, tiled=True, axis_index_groups=groups)  17.3 us
    all_to_all x1, blocking collectives, local(): lax.all_to_all(again, 'col', 0, 0, tiled=True, axis_index_groups=groups)  15.1 us
    pallas_call x1, Pallas kernels, pair_elements(): pl.pallas_call(pairs_kernel, out_shape=jax.ShapeDtypeStruct((rows, 128),...  13.3 us
    all_to_all x1, blocking collectives, local(): summands = lax.all_to_all(part, 'val', 0, 0, tiled=True)  11.5 us
    all_to_all x1, starting transfers between devices, local(): lax.all_to_all(half.reshape(chips, 7, 8, 128), 'col', 0, 0, tiled=True, a...  11 us
    all_to_all x1, waiting for transfers between devices, local(): lax.all_to_all(half.reshape(chips, 7, 8, 128), 'col', 0, 0, tiled=True, a...  7.8 us
    convert_element_type x1, other arithmetic, gather_words(): return (tile * 8, hot.astype(F32).astype(BF))  1.84 us
  transfers between devices with their start and end apart: 4, of which 3 were waited for; matrix products, arithmetic and copies ran while one was open for 5% of the time, Pallas kernels for 0%

profile of v4, /device:TPU:32, one launch (start us, length us, event | category | flops | bytes accessed | tf_op | source)
XLA Modules:
  0.0 88.3 jit_solution(5237987773048292501)
XLA Ops:
  0.0 0.0 copy-start.4
  0.0 0.0 copy-start.5
  0.0 1.2 %convert_element_type.33 = f16[1,1,2,48,2304]{4,3,2,1,0:T(8,128)(2,1)S(1)} convert(f32[1,1,2,48,2304]{4,3,2,1,0:T(8,128)} %param.10) | non-fusion elementwise | flops 221184 | bytes 1327104 | tf_op jit(solution)/shard_map/convert_element_type | solution.py:228
  1.2 0.1 fusion.4
  1.3 0.1 collective-permute-start
  1.4 0.7 select_reduce_fusion
  2.2 0.8 add_select_fusion
  3.0 0.0 collective-permute-done
  3.0 0.8 fusion.3
  3.8 11.0 %all-to-all-start = ((f16[16,7,8,128]{3,2,1,0:T(8,128)(2,1)}), f16[16,7,8,128]{3,2,1,0:T(8,128)(2,1)S(1)}, u32[]{:S(2)}, u32[]{:S(2)}) async-start(f16[16,7,8,128]{3,2,1,0:T(8,128)(2,1)} %bitcast.5), calls=%async_computation | async-start | bytes 458752 | tf_op jit(solution)/shard_map/all_to_all | solution.py:237
  14.8 1.8 %convert_convert_fusion.hot_ref = bf16[4096,128]{1,0:T(8,128)(2,1)S(1)} fusion(s32[4096]{0:T(1024)S(1)} %get-tuple-element.19), kind=kLoop, calls=%fused_computation | loop fusion | flops 1572864 | bytes 1064960 | tf_op jit(solution)/shard_map/convert_element_type | solution.py:215
  16.6 0.0 copy-start
  16.7 0.0 copy-start.1
  16.7 0.0 copy-start.2
  16.7 0.0 copy-start.3
  17.4 0.0 copy-done.4
  17.4 0.6 select_reduce_fusion.1
  18.7 0.0 copy-done.5
  18.7 7.8 %all-to-all-done = f16[16,7,8,128]{3,2,1,0:T(8,128)(2,1)S(1)} async-done(((f16[16,7,8,128]{3,2,1,0:T(8,128)(2,1)}), f16[16,7,8,128]{3,2,1,0:T(8,128)(2,1)S(1)}, u32[]{:S(2)}, u32[]{:S(2)}) %all-to-all-start) | async-done | bytes 229408 | tf_op jit(solution)/shard_map/all_to_all | solution.py:237
  26.5 0.1 broadcast_in_dim.70.scale_ref
  26.6 15.1 %all_to_all.20 = f16[16,7,8,128]{3,2,1,0:T(8,128)(2,1)S(1)} all-to-all(f16[16,7,8,128]{3,2,1,0:T(8,128)(2,1)S(1)} %broadcast_in_dim.72), channel_id=1, replica_groups={{0,2,4,6,8,10,12,14,16,18,20,22,24,26,28,30},{1,3,5,7,9,11,13,15,17,19,..., dimensions={0} | all-to-all | bytes 458752 | tf_op jit(solution)/shard_map/all_to_all | solution.py:246
  41.7 0.0 collective-permute-start.1
  41.7 1.5 %collective-permute-done.1 = f16[112,8,128]{2,1,0:T(8,128)(2,1)S(1)} collective-permute-done((f16[112,8,128]{2,1,0:T(8,128)(2,1)S(1)}, f16[112,8,128]{2,1,0:T(8,128)(2,1)S(1)}, u32[]{:S(2)}, u32[]{:S(2)}) %collective-permute-start.1) | collective-permute-done | bytes 229408 | tf_op jit(solution)/shard_map/ppermute | solution.py:247
  43.2 0.2 select_bitcast_fusion.1
  43.4 0.1 pad_maximum_fusion
  43.5 0.1 convert_bitcast_fusion.v_ref
  43.6 0.0 copy-done
  43.6 0.0 copy-done.1
  43.6 0.0 copy-done.2
  43.6 0.0 copy-done.3
  43.6 13.3 %pairs.1 = bf16[256,128]{1,0:T(8,128)(2,1)S(1)} custom-call(s32[4096]{0:T(1024)S(1)} %get-tuple-element.9.word_any, f32[4,2,48,2304]{3,2,1,0:T(8,128)} %c_any.1, f32[2,48,2304]{2,1,0:T(8,128)S(1)} %convert_bitcast_fusion.v_ref, f32[4,128]{1,0:T(4,128)S(1)} %broadcast_in_dim.70.scale_ref, f32[96,96]{1,0:T(8,128)S(1)} %copy-done.1, f32[2,48,384]{2,1,0:T(8,128)S(1)} %copy-done, ...), custom_call_target="tpu_custom_call" | custom-call | tf_op jit(solution)/shard_map/pairs/pallas_call | solution.py:186
  57.0 0.2 collective-permute-start.2
  57.2 1.1 %collective-permute-done.2 = bf16[20,8,128]{2,1,0:T(8,128)(2,1)S(1)} collective-permute-done((bf16[20,8,128]{2,1,0:T(8,128)(2,1)S(1)}, bf16[20,8,128]{2,1,0:T(8,128)(2,1)S(1)}, u32[]{:S(2)}, u32[]{:S(2)}) %collective-permute-start.2) | collective-permute-done | bytes 40992 | tf_op jit(solution)/shard_map/ppermute | solution.py:259
  58.4 17.3 %all_to_all.21 = bf16[16,10,8,128]{3,2,1,0:T(8,128)(2,1)S(1)} all-to-all(bf16[16,10,8,128]{3,2,1,0:T(8,128)(2,1)S(1)} %pad_maximum_fusion.1), channel_id=1, replica_groups={{0,2,4,6,8,10,12,14,16,18,20,22,24,26,28,30},{1,3,5,7,9,11,13,15,17,19,..., dimensions={0} | all-to-all | bytes 655360 | tf_op jit(solution)/shard_map/all_to_all | solution.py:264
  75.8 0.3 fusion.1
  76.1 11.5 %all_to_all.22 = bf16[8,64,256]{2,1,0:T(8,128)(2,1)S(1)} all-to-all(bf16[8,64,256]{2,1,0:T(8,128)(2,1)S(1)} %bitcast.61), channel_id=1, replica_groups=mesh['val'=8,'col'=32] {'val'}, dimensions={0} | all-to-all | bytes 524288 | tf_op jit(solution)/shard_map/all_to_all | solution.py:274
  87.7 0.6 copy.16
  (19 shorter events, 0.3 us)
Async XLA Ops:
  0.0 17.4 %copy-start.4 = (s32[8]{0:T(128)S(1)}, s32[8]{0:T(128)}, u32[]{:S(2)}) copy-start(s32[8]{0:T(128)} %param.11) | copy-start | bytes 100
  0.0 18.7 %copy-start.5 = (f32[4]{0:T(128)S(1)}, f32[4]{0:T(128)}, u32[]{:S(2)}) copy-start(f32[4]{0:T(128)} %param.14) | copy-start | bytes 52
  1.3 1.7 %collective-permute-start = (f16[112,8,128]{2,1,0:T(8,128)(2,1)S(1)}, f16[112,8,128]{2,1,0:T(8,128)(2,1)S(1)}, u32[]{:S(2)}, u32[]{:S(2)}) collective-permute-start(f16[112,8,128]{2,1,0:T(8,128)(2,1)S(1)} %fusion.4), channel_id=1, source_target_pairs={{0,1},{1,0},{2,3},{3,2},{4,5},{5,4},{6,7},{7,6},{8,9},{9,8},{10,11... | collective-permute-start | bytes 688136 | tf_op jit(solution)/shard_map/ppermute | solution.py:234
  3.8 22.8 %all-to-all-start = ((f16[16,7,8,128]{3,2,1,0:T(8,128)(2,1)}), f16[16,7,8,128]{3,2,1,0:T(8,128)(2,1)S(1)}, u32[]{:S(2)}, u32[]{:S(2)}) async-start(f16[16,7,8,128]{3,2,1,0:T(8,128)(2,1)} %bitcast.5), calls=%async_computation | async-start | bytes 458752 | tf_op jit(solution)/shard_map/all_to_all | solution.py:237
  16.6 26.9 %copy-start = (f32[2,48,384]{2,1,0:T(8,128)S(1)}, f32[2,48,384]{2,1,0:T(8,128)}, u32[]{:S(2)}) copy-start(f32[2,48,384]{2,1,0:T(8,128)} %constant.114.clone.t2a) | copy-start | bytes 442372
  16.7 26.9 %copy-start.1 = (f32[96,96]{1,0:T(8,128)S(1)}, f32[96,96]{1,0:T(8,128)}, u32[]{:S(2)}) copy-start(f32[96,96]{1,0:T(8,128)} %constant.113.clone.t1) | copy-start | bytes 110596
  16.7 26.9 %copy-start.2 = (f32[2,8,384]{2,1,0:T(8,128)S(1)}, f32[2,8,384]{2,1,0:T(8,128)}, u32[]{:S(2)}) copy-start(f32[2,8,384]{2,1,0:T(8,128)} %constant.116.clone.tw) | copy-start | bytes 73732
  16.7 26.9 %copy-start.3 = (f32[2,8,384]{2,1,0:T(8,128)S(1)}, f32[2,8,384]{2,1,0:T(8,128)}, u32[]{:S(2)}) copy-start(f32[2,8,384]{2,1,0:T(8,128)} %constant.115.clone.t2b) | copy-start | bytes 73732
  41.7 1.5 %collective-permute-start.1 = (f16[112,8,128]{2,1,0:T(8,128)(2,1)S(1)}, f16[112,8,128]{2,1,0:T(8,128)(2,1)S(1)}, u32[]{:S(2)}, u32[]{:S(2)}) collective-permute-start(f16[112,8,128]{2,1,0:T(8,128)(2,1)S(1)} %bitcast.60), channel_id=1, source_target_pairs={{0,1},{1,0},{2,3},{3,2},{4,5},{5,4},{6,7},{7,6},{8,9},{9,8},{10,11... | collective-permute-start | bytes 688136 | tf_op jit(solution)/shard_map/ppermute | solution.py:247
  57.0 1.3 %collective-permute-start.2 = (bf16[20,8,128]{2,1,0:T(8,128)(2,1)S(1)}, bf16[20,8,128]{2,1,0:T(8,128)(2,1)S(1)}, u32[]{:S(2)}, u32[]{:S(2)}) collective-permute-start(bf16[20,8,128]{2,1,0:T(8,128)(2,1)S(1)} %pad_maximum_fusion.2), channel_id=1, source_target_pairs={{0,1},{1,0},{2,3},{3,2},{4,5},{5,4},{6,7},{7,6},{8,9},{9,8},{10,11... | collective-permute-start | bytes 122888 | tf_op jit(solution)/shard_map/ppermute | solution.py:259

commit v5 on v4

--- a/solution.py
+++ b/solution.py
@@ -82,7 +82,7 @@
 
 
 def pairs_kernel(
-    word_any, c_any, v_ref, scale_ref, t1, t2a, t2b, tw, hot_ref, out_ref,
+    word_any, c_any, v_ref, scale_ref, t1, t2a, t2b, tw, spot_ref, out_ref,
     word, c_ref, a1, b2, p3, l2, grid, d0, d1, d2, d3, sems, word_sem,
 ):
     def fetch(band):
@@ -151,9 +151,14 @@
             start = pl.multiple_of(word[p * 256 + j], 8)
             d[h][pl.ds(i // 8 * 64 + i % 8, 8, stride=8), :] = grid[pl.ds(start, 8), :]
 
-    def partial_sum(p, d, k):
+    lane = lax.broadcasted_iota(jnp.int32, (128, 128), 1).astype(F32)
+
+    def one_hot(b):
+        spots = jnp.broadcast_to(spot_ref[b:b + 1, :], (128, 128)).T
+        return (spots == lane).astype(F32).astype(BF)
+
+    def partial_sum(p, d, k, hot):
         h, c0 = divmod(2 * k, 8)
-        hot = hot_ref[p * 256 + h * 128:p * 256 + h * 128 + 128, :]
         rows = []
         for c in (c0, c0 + 1):
             cell = jnp.concatenate([d[h][ib * 64 + c * 8:ib * 64 + c * 8 + 8, :] for ib in range(16)], 0)
@@ -170,14 +175,16 @@
     for p in range(count):
         total = None
         for k in range(8):
-            got = partial_sum(p, buffers[p % 2], k)
+            if k % 4 == 0:
+                hot = one_hot(2 * p + k // 4)
+            got = partial_sum(p, buffers[p % 2], k, hot)
             total = got if total is None else total + got
             if p + 1 < count:
                 copy(p + 1, buffers[(p + 1) % 2], 32 * k, 32 * k + 32)
         out_ref[p * 16:p * 16 + 16, :] = total.astype(BF)
 
 
-def pair_elements(valence, cond, scale, words, hot):
+def pair_elements(valence, cond, scale, words, spots):
     count = words.shape[0]
     rows = count // 128 * 8
     vmem = pl.BlockSpec(memory_space=pltpu.VMEM)
@@ -202,7 +209,7 @@
         ],
         compiler_params=pltpu.CompilerParams(vmem_limit_bytes=40 << 20),
         name="pairs",
-    )(words, cond, valence, scale, *tables(), hot)
+    )(words, cond, valence, scale, *tables(), spots)
 
 
 def gather_words(gvec_index):
@@ -211,8 +218,7 @@
     kz = gvec_index % L
     lane = ky // YB * L + kz
     tile = (ky % YB * L + kx) * 3 + lane // 128
-    hot = (lane % 128)[:, None] == lax.iota(jnp.int32, 128)[None, :]
-    return tile * 8, hot.astype(F32).astype(BF)
+    return tile * 8, (lane % 128).astype(F32).reshape(-1, 128)
 
 
 def local(valence_store, band_owner, valence_energy, cond_bands, cond_energy, gvec_index):
@@ -221,9 +227,8 @@
     chips = n_col // 2
     core = lax.axis_index("col") & 1
     bands = lax.iota(jnp.int32, band_owner.shape[0])
-    owner = jnp.sum(jnp.where(bands == lax.axis_index("val"), band_owner, 0))
     spread = jnp.broadcast_to(band_owner[:, None], (band_owner.shape[0], 128))
-    owner_core = jnp.sum(jnp.where(bands[:, None] == lax.axis_index("val"), spread, 0), 0) & 1
+    owner = jnp.sum(jnp.where(bands[:, None] == lax.axis_index("val"), spread, 0), 0)
 
     tiles = valence_store[0, 0].astype(jnp.float16).reshape(2, 6, 8, 18, 128)
     tiles = tiles.transpose(0, 1, 3, 2, 4).reshape(2, 108, 8, 128)
@@ -232,23 +237,24 @@
     mine = lax.dynamic_index_in_dim(tiles, core, 0, False)
     theirs = lax.dynamic_index_in_dim(tiles, 1 - core, 0, False)
     other = lax.ppermute(theirs, "col", swap)
-    half = jnp.where(owner_core[None, None, :] == core, mine, other)
+    half = jnp.where((owner & 1)[None, None, :] == core, mine, other)
+    source = lax.iota(jnp.int32, chips)[:, None] == (owner >> 1)[None, :]
+    half, words, spots, source = lax.optimization_barrier((half, *gather_words(gvec_index), source))
     groups = [[q * 2 + c for q in range(chips)] for c in range(2)]
     got = lax.all_to_all(half.reshape(chips, 7, 8, 128), "col", 0, 0, tiled=True, axis_index_groups=groups)
+    chunk = jnp.sum(jnp.where(source[:, None, None, :], got, 0).astype(F32), 0, keepdims=True)
+    again = jnp.broadcast_to(chunk.astype(got.dtype), (chips, 7, 8, 128))
+    half = lax.all_to_all(again, "col", 0, 0, tiled=True, axis_index_groups=groups).reshape(112, 8, 128)
+    half, cond_energy, valence_energy = lax.optimization_barrier((half, cond_energy, valence_energy))
+    other = lax.ppermute(half, "col", swap)
+    both = jnp.stack([jnp.where(core == 0, half, other), jnp.where(core == 0, other, half)], 0)
+    valence = both[:, :108].reshape(2, 6, 18, 8, 128).transpose(0, 1, 3, 2, 4).reshape(2, L, L * L).astype(F32)
+
     total_bands = cond_bands.shape[0] * n_col * n_val
     constant = total_bands ** (-0.25) * L ** (-1.5)
     scaling = jnp.sqrt(2.0 / (cond_energy - valence_energy[0])) * constant
     scale = jnp.broadcast_to(scaling[:, None], (scaling.shape[0], 128))
-    words, hot = gather_words(gvec_index)
-    chunk = lax.dynamic_index_in_dim(got, owner >> 1, 0, True)
-    chunk, scale, words, hot = lax.optimization_barrier((chunk, scale, words, hot))
-    again = jnp.broadcast_to(chunk, (chips, 7, 8, 128))
-    half = lax.all_to_all(again, "col", 0, 0, tiled=True, axis_index_groups=groups).reshape(112, 8, 128)
-    other = lax.ppermute(half, "col", swap)
-    both = jnp.stack([jnp.where(core == 0, half, other), jnp.where(core == 0, other, half)], 0)
-    valence = both[:, :108].reshape(2, 6, 18, 8, 128).transpose(0, 1, 3, 2, 4).reshape(2, L, L * L).astype(F32)
-
-    pairs = pair_elements(valence, cond_bands, scale, words, hot).reshape(n_col, 8, 128)
+    pairs = pair_elements(valence, cond_bands, scale, words, spots).reshape(n_col, 8, 128)
 
     row_count = ROW_DEV * n_val
     row_blocks = row_count // 128

time: 88.8 us -> 87.8 us (0.989)
  blocking collectives: 43.9 us -> 66.5 us
  starting transfers between devices: 11.4 us -> 0.32 us
  waiting for transfers between devices: 10.4 us -> 1.89 us
  other arithmetic: 6.49 us -> 3.4 us
    all_to_all x0 -> x1, blocking collectives: none -> 22.6 us  [local(): lax.all_to_all(half.reshape(chips, 7, 8, 128), 'col', 0, 0, tiled=True, a...]
    all_to_all x1 -> x0, starting transfers between devices: 11 us -> none  [local(): lax.all_to_all(half.reshape(chips, 7, 8, 128), 'col', 0, 0, tiled=True, a...]
    all_to_all x1 -> x0, waiting for transfers between devices: 7.8 us -> none  [local(): lax.all_to_all(half.reshape(chips, 7, 8, 128), 'col', 0, 0, tiled=True, a...]
    convert_element_type x1, other arithmetic: 1.84 us -> 0.01 us  [local(): again = jnp.broadcast_to(chunk.astype(got.dtype), (chips, 7, 8, 128))]
    select_n x2 -> x1, other arithmetic: 1.56 us -> 0.08 us  [local(): half = jnp.where((owner & 1)[None, None, :] == core, mine, other)]
  transfers between devices with their start and end apart: 4 -> 3, of which waited for: 3 -> 2; matrix products, arithmetic and copies ran while one was open for 5% -> 2% of each run, Pallas kernels for 0% -> 0%
where the time goes in v5:
time: 87.8 us; the launch traced here: 87.4 us
  blocking collectives  66.5 us (76%)
  Pallas kernels  13.2 us (15%)
  other arithmetic  3.4 us (4%)
  waiting for transfers between devices  1.89 us (2%)
  local copies, waits for them, and re-layouts  0.95 us (1%)
  between operations  0.88 us (1%)
    all_to_all x1, blocking collectives, local(): lax.all_to_all(half.reshape(chips, 7, 8, 128), 'col', 0, 0, tiled=True, a...  22.6 us
    all_to_all x1, blocking collectives, local(): lax.all_to_all(sent, 'col', 0, 0, tiled=True, axis_index_groups=groups)  17.3 us
    all_to_all x1, blocking collectives, local(): lax.all_to_all(again, 'col', 0, 0, tiled=True, axis_index_groups=groups)  15.1 us
    pallas_call x1, Pallas kernels, pair_elements(): pl.pallas_call(pairs_kernel, out_shape=jax.ShapeDtypeStruct((rows, 128),...  13.2 us
    all_to_all x1, blocking collectives, local(): summands = lax.all_to_all(part, 'val', 0, 0, tiled=True)  11.5 us
  transfers between devices with their start and end apart: 3, of which 2 were waited for; matrix products, arithmetic and copies ran while one was open for 2% of the time, Pallas kernels for 0%

profile of v5, /device:TPU:32, one launch (start us, length us, event | category | flops | bytes accessed | tf_op | source)
XLA Modules:
  0.0 87.4 jit_solution(3341161282596124073)
XLA Ops:
  0.0 0.0 copy-start.4
  0.0 0.0 copy-start
  0.0 0.0 copy-start.1
  0.0 0.0 copy-start.2
  0.0 0.0 copy-start.3
  0.0 1.3 %convert_element_type.43 = f16[1,1,2,48,2304]{4,3,2,1,0:T(8,128)(2,1)S(1)} convert(f32[1,1,2,48,2304]{4,3,2,1,0:T(8,128)} %param.10) | non-fusion elementwise | flops 221184 | bytes 1327104 | tf_op jit(solution)/shard_map/convert_element_type | solution.py:233
  1.3 0.1 fusion.4
  1.4 0.1 collective-permute-start
  1.5 0.7 select_reduce_fusion
  2.3 0.8 fusion.18
  3.1 0.0 collective-permute-done
  3.1 0.1 fusion.3
  3.2 22.6 %all_to_all.20 = f16[16,7,8,128]{3,2,1,0:T(8,128)(2,1)S(1)} all-to-all(f16[16,7,8,128]{3,2,1,0:T(8,128)(2,1)S(1)} %bitcast.61), channel_id=1, replica_groups={{0,2,4,6,8,10,12,14,16,18,20,22,24,26,28,30},{1,3,5,7,9,11,13,15,17,19,..., dimensions={0} | all-to-all | bytes 458752 | tf_op jit(solution)/shard_map/all_to_all | solution.py:244
  25.7 0.1 convert_reduce_fusion.1
  25.8 15.1 %all_to_all.21 = f16[16,7,8,128]{3,2,1,0:T(8,128)(2,1)S(1)} all-to-all(f16[16,7,8,128]{3,2,1,0:T(8,128)(2,1)S(1)} %broadcast_in_dim.79), channel_id=1, replica_groups={{0,2,4,6,8,10,12,14,16,18,20,22,24,26,28,30},{1,3,5,7,9,11,13,15,17,19,..., dimensions={0} | all-to-all | bytes 458752 | tf_op jit(solution)/shard_map/all_to_all | solution.py:247
  40.9 0.0 collective-permute-start.1
  41.6 0.0 copy-done.4
  41.6 0.8 collective-permute-done.1
  42.4 0.1 select_bitcast_fusion.1
  42.6 0.1 pad_maximum_fusion
  42.7 0.1 convert_bitcast_fusion.v_ref
  42.7 0.1 broadcast_in_dim.80.scale_ref
  42.8 0.0 copy-done
  42.8 0.0 copy-done.1
  42.8 0.0 copy-done.2
  42.8 0.0 copy-done.3
  42.8 13.2 %pairs.1 = bf16[256,128]{1,0:T(8,128)(2,1)S(1)} custom-call(s32[4096]{0:T(1024)S(1)} %get-tuple-element.12.word_any, f32[4,2,48,2304]{3,2,1,0:T(8,128)} %c_any.1, f32[2,48,2304]{2,1,0:T(8,128)S(1)} %convert_bitcast_fusion.v_ref, f32[4,128]{1,0:T(4,128)S(1)} %broadcast_in_dim.80.scale_ref, f32[96,96]{1,0:T(8,128)S(1)} %copy-done.1, ...), custom_call_target="tpu_custom_call" | custom-call | tf_op jit(solution)/shard_map/pairs/pallas_call | solution.py:193
  56.1 0.2 collective-permute-start.2
  56.3 1.1 %collective-permute-done.2 = bf16[20,8,128]{2,1,0:T(8,128)(2,1)S(1)} collective-permute-done((bf16[20,8,128]{2,1,0:T(8,128)(2,1)S(1)}, bf16[20,8,128]{2,1,0:T(8,128)(2,1)S(1)}, u32[]{:S(2)}, u32[]{:S(2)}) %collective-permute-start.2) | collective-permute-done | bytes 40992 | tf_op jit(solution)/shard_map/ppermute | solution.py:265
  57.5 17.3 %all_to_all.22 = bf16[16,10,8,128]{3,2,1,0:T(8,128)(2,1)S(1)} all-to-all(bf16[16,10,8,128]{3,2,1,0:T(8,128)(2,1)S(1)} %pad_maximum_fusion.1), channel_id=1, replica_groups={{0,2,4,6,8,10,12,14,16,18,20,22,24,26,28,30},{1,3,5,7,9,11,13,15,17,19,..., dimensions={0} | all-to-all | bytes 655360 | tf_op jit(solution)/shard_map/all_to_all | solution.py:270
  74.9 0.3 fusion.1
  75.2 11.5 %all_to_all.23 = bf16[8,64,256]{2,1,0:T(8,128)(2,1)S(1)} all-to-all(bf16[8,64,256]{2,1,0:T(8,128)(2,1)S(1)} %bitcast.62), channel_id=1, replica_groups=mesh['val'=8,'col'=32] {'val'}, dimensions={0} | all-to-all | bytes 524288 | tf_op jit(solution)/shard_map/all_to_all | solution.py:280
  86.8 0.6 copy.16
  (21 shorter events, 0.3 us)
Async XLA Ops:
  0.0 41.6 %copy-start.4 = (f32[4]{0:T(128)S(1)}, f32[4]{0:T(128)}, u32[]{:S(2)}) copy-start(f32[4]{0:T(128)} %param.14) | copy-start | bytes 52
  0.0 42.8 %copy-start = (f32[2,48,384]{2,1,0:T(8,128)S(1)}, f32[2,48,384]{2,1,0:T(8,128)}, u32[]{:S(2)}) copy-start(f32[2,48,384]{2,1,0:T(8,128)} %constant.109.clone.t2a) | copy-start | bytes 442372
  0.0 42.8 %copy-start.1 = (f32[96,96]{1,0:T(8,128)S(1)}, f32[96,96]{1,0:T(8,128)}, u32[]{:S(2)}) copy-start(f32[96,96]{1,0:T(8,128)} %constant.108.clone.t1) | copy-start | bytes 110596
  0.0 42.8 %copy-start.2 = (f32[2,8,384]{2,1,0:T(8,128)S(1)}, f32[2,8,384]{2,1,0:T(8,128)}, u32[]{:S(2)}) copy-start(f32[2,8,384]{2,1,0:T(8,128)} %constant.110.clone.t2b) | copy-start | bytes 73732
  0.0 42.8 %copy-start.3 = (f32[2,8,384]{2,1,0:T(8,128)S(1)}, f32[2,8,384]{2,1,0:T(8,128)}, u32[]{:S(2)}) copy-start(f32[2,8,384]{2,1,0:T(8,128)} %constant.111.clone.tw) | copy-start | bytes 73732
  1.4 1.7 %collective-permute-start = (f16[112,8,128]{2,1,0:T(8,128)(2,1)S(1)}, f16[112,8,128]{2,1,0:T(8,128)(2,1)S(1)}, u32[]{:S(2)}, u32[]{:S(2)}) collective-permute-start(f16[112,8,128]{2,1,0:T(8,128)(2,1)S(1)} %fusion.4), channel_id=1, source_target_pairs={{0,1},{1,0},{2,3},{3,2},{4,5},{5,4},{6,7},{7,6},{8,9},{9,8},{10,11... | collective-permute-start | bytes 688136 | tf_op jit(solution)/shard_map/ppermute | solution.py:239
  40.9 1.5 %collective-permute-start.1 = (f16[112,8,128]{2,1,0:T(8,128)(2,1)S(1)}, f16[112,8,128]{2,1,0:T(8,128)(2,1)S(1)}, u32[]{:S(2)}, u32[]{:S(2)}) collective-permute-start(f16[112,8,128]{2,1,0:T(8,128)(2,1)S(1)} %bitcast.59), channel_id=1, source_target_pairs={{0,1},{1,0},{2,3},{3,2},{4,5},{5,4},{6,7},{7,6},{8,9},{9,8},{10,11... | collective-permute-start | bytes 688136 | tf_op jit(solution)/shard_map/ppermute | solution.py:249
  56.1 1.3 %collective-permute-start.2 = (bf16[20,8,128]{2,1,0:T(8,128)(2,1)S(1)}, bf16[20,8,128]{2,1,0:T(8,128)(2,1)S(1)}, u32[]{:S(2)}, u32[]{:S(2)}) collective-permute-start(bf16[20,8,128]{2,1,0:T(8,128)(2,1)S(1)} %pad_maximum_fusion.2), channel_id=1, source_target_pairs={{0,1},{1,0},{2,3},{3,2},{4,5},{5,4},{6,7},{7,6},{8,9},{9,8},{10,11... | collective-permute-start | bytes 122888 | tf_op jit(solution)/shard_map/ppermute | solution.py:265

commit v6 on v5

--- a/solution.py
+++ b/solution.py
@@ -230,20 +230,25 @@
     spread = jnp.broadcast_to(band_owner[:, None], (band_owner.shape[0], 128))
     owner = jnp.sum(jnp.where(bands[:, None] == lax.axis_index("val"), spread, 0), 0)
 
-    tiles = valence_store[0, 0].astype(jnp.float16).reshape(2, 6, 8, 18, 128)
-    tiles = tiles.transpose(0, 1, 3, 2, 4).reshape(2, 108, 8, 128)
-    tiles = jnp.pad(tiles, ((0, 0), (0, 4), (0, 0), (0, 0)))
+    def component(field, index):
+        tiles = field.reshape(2, 6, 8, 18, 128).transpose(0, 1, 3, 2, 4).reshape(2, 108, 8, 128)
+        picked = lax.dynamic_index_in_dim(tiles, index, 0, False).astype(jnp.float16)
+        return jnp.pad(picked, ((0, 4), (0, 0), (0, 0)))
+
     swap = [(i, i ^ 1) for i in range(n_col)]
-    mine = lax.dynamic_index_in_dim(tiles, core, 0, False)
-    theirs = lax.dynamic_index_in_dim(tiles, 1 - core, 0, False)
+    theirs = component(valence_store[0, 0], 1 - core)
     other = lax.ppermute(theirs, "col", swap)
+    mine = lax.optimization_barrier(component(lax.optimization_barrier(valence_store)[0, 0], core))
     half = jnp.where((owner & 1)[None, None, :] == core, mine, other)
     source = lax.iota(jnp.int32, chips)[:, None] == (owner >> 1)[None, :]
-    half, words, spots, source = lax.optimization_barrier((half, *gather_words(gvec_index), source))
+    half, source = lax.optimization_barrier((half, source))
     groups = [[q * 2 + c for q in range(chips)] for c in range(2)]
     got = lax.all_to_all(half.reshape(chips, 7, 8, 128), "col", 0, 0, tiled=True, axis_index_groups=groups)
+    got, gvec_index = lax.optimization_barrier((got, gvec_index))
+    words, spots = gather_words(gvec_index)
     chunk = jnp.sum(jnp.where(source[:, None, None, :], got, 0).astype(F32), 0, keepdims=True)
     again = jnp.broadcast_to(chunk.astype(got.dtype), (chips, 7, 8, 128))
+    again, words, spots = lax.optimization_barrier((again, words, spots))
     half = lax.all_to_all(again, "col", 0, 0, tiled=True, axis_index_groups=groups).reshape(112, 8, 128)
     half, cond_energy, valence_energy = lax.optimization_barrier((half, cond_energy, valence_energy))
     other = lax.ppermute(half, "col", swap)

time: 87.8 us -> 88 us (level)
    convert_element_type x1 -> x2, other arithmetic: 1.27 us -> 2.12 us  [component(): lax.dynamic_index_in_dim(tiles, index, 0, False).astype(jnp.float16)]
where the time goes in v6:
time: 88 us; the launch traced here: 87.7 us
  blocking collectives  66.5 us (76%)
  Pallas kernels  13.2 us (15%)
  other arithmetic  3.52 us (4%)
  waiting for transfers between devices  1.9 us (2%)
  local copies, waits for them, and re-layouts  1 us (1%)
  between operations  0.92 us (1%)
    all_to_all x1, blocking collectives, local(): lax.all_to_all(half.reshape(chips, 7, 8, 128), 'col', 0, 0, tiled=True, a...  22.6 us
    all_to_all x1, blocking collectives, local(): lax.all_to_all(sent, 'col', 0, 0, tiled=True, axis_index_groups=groups)  17.3 us
    all_to_all x1, blocking collectives, local(): lax.all_to_all(again, 'col', 0, 0, tiled=True, axis_index_groups=groups)  15.1 us
    pallas_call x1, Pallas kernels, pair_elements(): pl.pallas_call(pairs_kernel, out_shape=jax.ShapeDtypeStruct((rows, 128),...  13.2 us
    all_to_all x1, blocking collectives, local(): summands = lax.all_to_all(part, 'val', 0, 0, tiled=True)  11.5 us
    convert_element_type x2, other arithmetic, component(): lax.dynamic_index_in_dim(tiles, index, 0, False).astype(jnp.float16)  2.12 us
  transfers between devices with their start and end apart: 3, of which 2 were waited for; matrix products, arithmetic and copies ran while one was open for 2% of the time, Pallas kernels for 0%

profile of v6, /device:TPU:32, one launch (start us, length us, event | category | flops | bytes accessed | tf_op | source)
XLA Modules:
  0.0 87.7 jit_solution(1392236403699512457)
XLA Ops:
  0.0 0.0 copy-start.4
  0.0 0.0 copy-start.5
  0.0 1.1 %fusion.3 = f16[108,8,128]{2,1,0:T(8,128)(2,1)S(1)} fusion(f32[2,108,8,128]{3,2,1,0:T(8,128)} %bitcast.63, s32[]{:T(128)S(6)} %select_n.69), kind=kLoop, calls=%fused_computation.15 | loop fusion | flops 110592 | bytes 663556 | tf_op jit(solution)/shard_map/convert_element_type | solution.py:235
  1.1 0.0 copy-start
  1.1 0.0 copy-start.1
  1.1 0.0 copy-start.2
  1.1 0.0 copy-start.3
  1.2 0.1 collective-permute-start
  1.3 0.7 select_reduce_fusion
  2.1 1.1 %fusion.2 = f16[108,8,128]{2,1,0:T(8,128)(2,1)S(1)} fusion(f32[2,108,8,128]{3,2,1,0:T(8,128)} %bitcast.64, s32[]{:T(128)S(6)} %select_n.68), kind=kLoop, calls=%fused_computation.14 | loop fusion | flops 110592 | bytes 663556 | tf_op jit(solution)/shard_map/convert_element_type | solution.py:235
  3.2 0.0 collective-permute-done
  3.2 0.1 broadcast_select_fusion
  3.3 22.6 %all_to_all.20 = f16[16,7,8,128]{3,2,1,0:T(8,128)(2,1)S(1)} all-to-all(f16[16,7,8,128]{3,2,1,0:T(8,128)(2,1)S(1)} %bitcast.62), channel_id=1, replica_groups={{0,2,4,6,8,10,12,14,16,18,20,22,24,26,28,30},{1,3,5,7,9,11,13,15,17,19,..., dimensions={0} | all-to-all | bytes 458752 | tf_op jit(solution)/shard_map/all_to_all | solution.py:246
  25.9 0.1 convert_reduce_fusion.1
  25.9 0.0 copy-done.4
  25.9 0.1 fusion.17
  26.1 15.1 %all_to_all.21 = f16[16,7,8,128]{3,2,1,0:T(8,128)(2,1)S(1)} all-to-all(f16[16,7,8,128]{3,2,1,0:T(8,128)(2,1)S(1)} %broadcast_in_dim.79), channel_id=1, replica_groups={{0,2,4,6,8,10,12,14,16,18,20,22,24,26,28,30},{1,3,5,7,9,11,13,15,17,19,..., dimensions={0} | all-to-all | bytes 458752 | tf_op jit(solution)/shard_map/all_to_all | solution.py:252
  41.2 0.0 collective-permute-start.1
  41.8 0.0 copy-done.5
  41.8 0.8 collective-permute-done.1
  42.6 0.1 select_bitcast_fusion.1
  42.8 0.1 pad_maximum_fusion
  42.9 0.1 convert_bitcast_fusion.v_ref
  43.0 0.1 broadcast_in_dim.80.scale_ref
  43.0 0.0 copy-done
  43.0 0.0 copy-done.1
  43.0 0.0 copy-done.2
  43.0 0.0 copy-done.3
  43.0 13.2 %pairs.1 = bf16[256,128]{1,0:T(8,128)(2,1)S(1)} custom-call(s32[4096]{0:T(1024)S(1)} %get-tuple-element.19.word_any, f32[4,2,48,2304]{3,2,1,0:T(8,128)} %c_any.1, f32[2,48,2304]{2,1,0:T(8,128)S(1)} %convert_bitcast_fusion.v_ref, f32[4,128]{1,0:T(4,128)S(1)} %broadcast_in_dim.80.scale_ref, f32[96,96]{1,0:T(8,128)S(1)} %copy-done.1, ...), custom_call_target="tpu_custom_call" | custom-call | tf_op jit(solution)/shard_map/pairs/pallas_call | solution.py:193
  56.3 0.2 collective-permute-start.2
  56.5 1.1 %collective-permute-done.2 = bf16[20,8,128]{2,1,0:T(8,128)(2,1)S(1)} collective-permute-done((bf16[20,8,128]{2,1,0:T(8,128)(2,1)S(1)}, bf16[20,8,128]{2,1,0:T(8,128)(2,1)S(1)}, u32[]{:S(2)}, u32[]{:S(2)}) %collective-permute-start.2) | collective-permute-done | bytes 40992 | tf_op jit(solution)/shard_map/ppermute | solution.py:270
  57.7 17.3 %all_to_all.22 = bf16[16,10,8,128]{3,2,1,0:T(8,128)(2,1)S(1)} all-to-all(bf16[16,10,8,128]{3,2,1,0:T(8,128)(2,1)S(1)} %pad_maximum_fusion.1), channel_id=1, replica_groups={{0,2,4,6,8,10,12,14,16,18,20,22,24,26,28,30},{1,3,5,7,9,11,13,15,17,19,..., dimensions={0} | all-to-all | bytes 655360 | tf_op jit(solution)/shard_map/all_to_all | solution.py:275
  75.1 0.3 fusion.1
  75.4 11.5 %all_to_all.23 = bf16[8,64,256]{2,1,0:T(8,128)(2,1)S(1)} all-to-all(bf16[8,64,256]{2,1,0:T(8,128)(2,1)S(1)} %bitcast.65), channel_id=1, replica_groups=mesh['val'=8,'col'=32] {'val'}, dimensions={0} | all-to-all | bytes 524288 | tf_op jit(solution)/shard_map/all_to_all | solution.py:285
  87.0 0.6 copy.16
  (23 shorter events, 0.4 us)
Async XLA Ops:
  0.0 25.9 %copy-start.4 = (s32[4096]{0:T(1024)S(1)}, s32[4096]{0:T(1024)}, u32[]{:S(2)}) copy-start(s32[4096]{0:T(1024)} %param.15) | copy-start | bytes 49156
  0.0 41.8 %copy-start.5 = (f32[4]{0:T(128)S(1)}, f32[4]{0:T(128)}, u32[]{:S(2)}) copy-start(f32[4]{0:T(128)} %param.14) | copy-start | bytes 52
  1.1 42.0 %copy-start = (f32[2,48,384]{2,1,0:T(8,128)S(1)}, f32[2,48,384]{2,1,0:T(8,128)}, u32[]{:S(2)}) copy-start(f32[2,48,384]{2,1,0:T(8,128)} %constant.109.clone.t2a) | copy-start | bytes 442372
  1.1 41.9 %copy-start.1 = (f32[96,96]{1,0:T(8,128)S(1)}, f32[96,96]{1,0:T(8,128)}, u32[]{:S(2)}) copy-start(f32[96,96]{1,0:T(8,128)} %constant.108.clone.t1) | copy-start | bytes 110596
  1.1 41.9 %copy-start.2 = (f32[2,8,384]{2,1,0:T(8,128)S(1)}, f32[2,8,384]{2,1,0:T(8,128)}, u32[]{:S(2)}) copy-start(f32[2,8,384]{2,1,0:T(8,128)} %constant.110.clone.t2b) | copy-start | bytes 73732
  1.1 41.9 %copy-start.3 = (f32[2,8,384]{2,1,0:T(8,128)S(1)}, f32[2,8,384]{2,1,0:T(8,128)}, u32[]{:S(2)}) copy-start(f32[2,8,384]{2,1,0:T(8,128)} %constant.111.clone.tw) | copy-start | bytes 73732
  1.2 2.0 %collective-permute-start = (f16[112,8,128]{2,1,0:T(8,128)(2,1)S(1)}, f16[112,8,128]{2,1,0:T(8,128)(2,1)S(1)}, u32[]{:S(2)}, u32[]{:S(2)}) collective-permute-start(f16[112,8,128]{2,1,0:T(8,128)(2,1)S(1)} %pad.8), channel_id=1, source_target_pairs={{0,1},{1,0},{2,3},{3,2},{4,5},{5,4},{6,7},{7,6},{8,9},{9,8},{10,11... | collective-permute-start | bytes 688136 | tf_op jit(solution)/shard_map/ppermute | solution.py:240
  41.2 1.5 %collective-permute-start.1 = (f16[112,8,128]{2,1,0:T(8,128)(2,1)S(1)}, f16[112,8,128]{2,1,0:T(8,128)(2,1)S(1)}, u32[]{:S(2)}, u32[]{:S(2)}) collective-permute-start(f16[112,8,128]{2,1,0:T(8,128)(2,1)S(1)} %bitcast.60), channel_id=1, source_target_pairs={{0,1},{1,0},{2,3},{3,2},{4,5},{5,4},{6,7},{7,6},{8,9},{9,8},{10,11... | collective-permute-start | bytes 688136 | tf_op jit(solution)/shard_map/ppermute | solution.py:254
  56.3 1.3 %collective-permute-start.2 = (bf16[20,8,128]{2,1,0:T(8,128)(2,1)S(1)}, bf16[20,8,128]{2,1,0:T(8,128)(2,1)S(1)}, u32[]{:S(2)}, u32[]{:S(2)}) collective-permute-start(bf16[20,8,128]{2,1,0:T(8,128)(2,1)S(1)} %pad_maximum_fusion.2), channel_id=1, source_target_pairs={{0,1},{1,0},{2,3},{3,2},{4,5},{5,4},{6,7},{7,6},{8,9},{9,8},{10,11... | collective-permute-start | bytes 122888 | tf_op jit(solution)/shard_map/ppermute | solution.py:270

commit v7 on v6

--- a/solution.py
+++ b/solution.py
@@ -83,7 +83,7 @@
 
 def pairs_kernel(
     word_any, c_any, v_ref, scale_ref, t1, t2a, t2b, tw, spot_ref, out_ref,
-    word, c_ref, a1, b2, p3, l2, grid, d0, d1, d2, d3, sems, word_sem,
+    word, c_ref, a1, b2, p3, l2, grid, hots, wide, sems, word_sem,
 ):
     def fetch(band):
         return pltpu.make_async_copy(c_any.at[band], c_ref.at[band], sems.at[band])
@@ -141,47 +141,29 @@
 
     lax.fori_loop(0, 2, bands, 0)
 
-    row = lax.broadcasted_iota(jnp.int32, (16, 8 * 128), 0)
-    comp = lax.broadcasted_iota(jnp.int32, (16, 8 * 128), 1) // 128
-    pick = [(row == comp + 8 * h).astype(F32).astype(BF) for h in range(2)]
-
-    def copy(p, d, first, last):
-        for j in range(first, last):
-            h, i = divmod(j, 128)
-            start = pl.multiple_of(word[p * 256 + j], 8)
-            d[h][pl.ds(i // 8 * 64 + i % 8, 8, stride=8), :] = grid[pl.ds(start, 8), :]
-
     lane = lax.broadcasted_iota(jnp.int32, (128, 128), 1).astype(F32)
-
-    def one_hot(b):
-        spots = jnp.broadcast_to(spot_ref[b:b + 1, :], (128, 128)).T
-        return (spots == lane).astype(F32).astype(BF)
-
-    def partial_sum(p, d, k, hot):
-        h, c0 = divmod(2 * k, 8)
-        rows = []
-        for c in (c0, c0 + 1):
-            cell = jnp.concatenate([d[h][ib * 64 + c * 8:ib * 64 + c * 8 + 8, :] for ib in range(16)], 0)
-            rows.append(cell.astype(BF) * hot)
-        return lax.dot_general(
-            pick[h][:, c0 * 128:c0 * 128 + 256], jnp.concatenate(rows, 1),
-            (((1,), (1,)), ((), ())), preferred_element_type=F32,
-        )
+    own = lax.broadcasted_iota(jnp.int32, (8, 256), 1) % 8 == lax.broadcasted_iota(jnp.int32, (8, 256), 0)
+    ones = jnp.ones((16, 128), BF)
 
     word_copy.wait()
-    buffers = (d0, d1), (d2, d3)
-    count = out_ref.shape[0] // 16
-    copy(0, buffers[0], 0, 256)
-    for p in range(count):
-        total = None
-        for k in range(8):
-            if k % 4 == 0:
-                hot = one_hot(2 * p + k // 4)
-            got = partial_sum(p, buffers[p % 2], k, hot)
-            total = got if total is None else total + got
-            if p + 1 < count:
-                copy(p + 1, buffers[(p + 1) % 2], 32 * k, 32 * k + 32)
-        out_ref[p * 16:p * 16 + 16, :] = total.astype(BF)
+    for b in range(spot_ref.shape[0]):
+        hot = hots.at[b % 2]
+        hot[...] = (jnp.broadcast_to(spot_ref[b:b + 1, :], (128, 128)).T == lane).astype(F32)
+        for j in range(4):
+            rows = []
+            for i in range(32 * j, 32 * j + 32):
+                start = pl.multiple_of(word[b * 128 + i], 8)
+                rows.append(grid[pl.ds(start, 8), :] * jnp.broadcast_to(hot[i:i + 1, :], (8, 128)))
+            sums = lax.dot_general(
+                ones, jnp.concatenate(rows, 0).astype(BF),
+                (((1,), (1,)), ((), ())), preferred_element_type=F32,
+            )
+            wide[b * 8:b * 8 + 8, j * 256:j * 256 + 256] = jnp.where(own, sums[:8], 0.0)
+    fold = (
+        lax.broadcasted_iota(jnp.int32, (1024, 128), 0) // 8
+        == lax.broadcasted_iota(jnp.int32, (1024, 128), 1)
+    ).astype(F32).astype(BF)
+    out_ref[...] = jnp.dot(wide[...].astype(BF), fold, preferred_element_type=F32).astype(BF)
 
 
 def pair_elements(valence, cond, scale, words, spots):
@@ -203,7 +185,8 @@
             pltpu.VMEM((YB, K1, 2 * SLAB), BF),
             pltpu.VMEM((2 * R1, K2), BF),
             pltpu.VMEM((R1 * 24, 128), F32),
-        ] + [pltpu.VMEM((8 * 128, 128), F32)] * 4 + [
+            pltpu.VMEM((2, 128, 128), F32),
+            pltpu.VMEM((rows, 1024), F32),
             pltpu.SemaphoreType.DMA((cond.shape[0],)),
             pltpu.SemaphoreType.DMA(()),
         ],

time: 88 us -> 86.7 us (0.985)
  Pallas kernels: 13.2 us -> 11.9 us
    pallas_call x1, Pallas kernels: 13.2 us -> 11.9 us  [pair_elements(): pl.pallas_call(pairs_kernel, out_shape=jax.ShapeDtypeStruct((rows, 128),...]
where the time goes in v7:
time: 86.7 us; the launch traced here: 86.4 us
  blocking collectives  66.5 us (77%)
  Pallas kernels  11.9 us (14%)
  other arithmetic  3.52 us (4%)
  waiting for transfers between devices  1.89 us (2%)
  local copies, waits for them, and re-layouts  1 us (1%)
  between operations  0.92 us (1%)
    all_to_all x1, blocking collectives, local(): lax.all_to_all(half.reshape(chips, 7, 8, 128), 'col', 0, 0, tiled=True, a...  22.6 us
    all_to_all x1, blocking collectives, local(): lax.all_to_all(sent, 'col', 0, 0, tiled=True, axis_index_groups=groups)  17.3 us
    all_to_all x1, blocking collectives, local(): lax.all_to_all(again, 'col', 0, 0, tiled=True, axis_index_groups=groups)  15.1 us
    pallas_call x1, Pallas kernels, pair_elements(): pl.pallas_call(pairs_kernel, out_shape=jax.ShapeDtypeStruct((rows, 128),...  11.9 us
    all_to_all x1, blocking collectives, local(): summands = lax.all_to_all(part, 'val', 0, 0, tiled=True)  11.5 us
    convert_element_type x2, other arithmetic, component(): lax.dynamic_index_in_dim(tiles, index, 0, False).astype(jnp.float16)  2.12 us
  transfers between devices with their start and end apart: 3, of which 2 were waited for; matrix products, arithmetic and copies ran while one was open for 2% of the time, Pallas kernels for 0%

profile of v7, /device:TPU:32, one launch (start us, length us, event | category | flops | bytes accessed | tf_op | source)
XLA Modules:
  0.0 86.4 jit_solution(2169361530950312203)
XLA Ops:
  0.0 0.0 copy-start.4
  0.0 0.0 copy-start.5
  0.0 1.1 %fusion.3 = f16[108,8,128]{2,1,0:T(8,128)(2,1)S(1)} fusion(f32[2,108,8,128]{3,2,1,0:T(8,128)} %bitcast.63, s32[]{:T(128)S(6)} %select_n.69), kind=kLoop, calls=%fused_computation.15 | loop fusion | flops 110592 | bytes 663556 | tf_op jit(solution)/shard_map/convert_element_type | solution.py:218
  1.1 0.0 copy-start
  1.1 0.0 copy-start.1
  1.1 0.0 copy-start.2
  1.1 0.0 copy-start.3
  1.2 0.1 collective-permute-start
  1.3 0.7 select_reduce_fusion
  2.1 1.1 %fusion.2 = f16[108,8,128]{2,1,0:T(8,128)(2,1)S(1)} fusion(f32[2,108,8,128]{3,2,1,0:T(8,128)} %bitcast.64, s32[]{:T(128)S(6)} %select_n.68), kind=kLoop, calls=%fused_computation.14 | loop fusion | flops 110592 | bytes 663556 | tf_op jit(solution)/shard_map/convert_element_type | solution.py:218
  3.2 0.0 collective-permute-done
  3.2 0.1 broadcast_select_fusion
  3.3 22.6 %all_to_all.20 = f16[16,7,8,128]{3,2,1,0:T(8,128)(2,1)S(1)} all-to-all(f16[16,7,8,128]{3,2,1,0:T(8,128)(2,1)S(1)} %bitcast.62), channel_id=1, replica_groups={{0,2,4,6,8,10,12,14,16,18,20,22,24,26,28,30},{1,3,5,7,9,11,13,15,17,19,..., dimensions={0} | all-to-all | bytes 458752 | tf_op jit(solution)/shard_map/all_to_all | solution.py:229
  25.9 0.1 convert_reduce_fusion.1
  25.9 0.0 copy-done.4
  25.9 0.1 fusion.17
  26.1 15.1 %all_to_all.21 = f16[16,7,8,128]{3,2,1,0:T(8,128)(2,1)S(1)} all-to-all(f16[16,7,8,128]{3,2,1,0:T(8,128)(2,1)S(1)} %broadcast_in_dim.79), channel_id=1, replica_groups={{0,2,4,6,8,10,12,14,16,18,20,22,24,26,28,30},{1,3,5,7,9,11,13,15,17,19,..., dimensions={0} | all-to-all | bytes 458752 | tf_op jit(solution)/shard_map/all_to_all | solution.py:235
  41.2 0.0 collective-permute-start.1
  41.8 0.0 copy-done.5
  41.8 0.8 collective-permute-done.1
  42.6 0.1 select_bitcast_fusion.1
  42.8 0.1 pad_maximum_fusion
  42.9 0.1 convert_bitcast_fusion.v_ref
  43.0 0.1 broadcast_in_dim.80.scale_ref
  43.0 0.0 copy-done
  43.0 0.0 copy-done.1
  43.0 0.0 copy-done.2
  43.0 0.0 copy-done.3
  43.0 11.9 %pairs.1 = bf16[256,128]{1,0:T(8,128)(2,1)S(1)} custom-call(s32[4096]{0:T(1024)S(1)} %get-tuple-element.19.word_any, f32[4,2,48,2304]{3,2,1,0:T(8,128)} %c_any.1, f32[2,48,2304]{2,1,0:T(8,128)S(1)} %convert_bitcast_fusion.v_ref, f32[4,128]{1,0:T(4,128)S(1)} %broadcast_in_dim.80.scale_ref, f32[96,96]{1,0:T(8,128)S(1)} %copy-done.1, ...), custom_call_target="tpu_custom_call" | custom-call | tf_op jit(solution)/shard_map/pairs/pallas_call | solution.py:175
  55.0 0.2 collective-permute-start.2
  55.3 1.1 %collective-permute-done.2 = bf16[20,8,128]{2,1,0:T(8,128)(2,1)S(1)} collective-permute-done((bf16[20,8,128]{2,1,0:T(8,128)(2,1)S(1)}, bf16[20,8,128]{2,1,0:T(8,128)(2,1)S(1)}, u32[]{:S(2)}, u32[]{:S(2)}) %collective-permute-start.2) | collective-permute-done | bytes 40992 | tf_op jit(solution)/shard_map/ppermute | solution.py:253
  56.5 17.3 %all_to_all.22 = bf16[16,10,8,128]{3,2,1,0:T(8,128)(2,1)S(1)} all-to-all(bf16[16,10,8,128]{3,2,1,0:T(8,128)(2,1)S(1)} %pad_maximum_fusion.1), channel_id=1, replica_groups={{0,2,4,6,8,10,12,14,16,18,20,22,24,26,28,30},{1,3,5,7,9,11,13,15,17,19,..., dimensions={0} | all-to-all | bytes 655360 | tf_op jit(solution)/shard_map/all_to_all | solution.py:258
  73.9 0.3 fusion.1
  74.2 11.5 %all_to_all.23 = bf16[8,64,256]{2,1,0:T(8,128)(2,1)S(1)} all-to-all(bf16[8,64,256]{2,1,0:T(8,128)(2,1)S(1)} %bitcast.65), channel_id=1, replica_groups=mesh['val'=8,'col'=32] {'val'}, dimensions={0} | all-to-all | bytes 524288 | tf_op jit(solution)/shard_map/all_to_all | solution.py:268
  85.8 0.6 copy.16
  (23 shorter events, 0.4 us)
Async XLA Ops:
  0.0 25.9 %copy-start.4 = (s32[4096]{0:T(1024)S(1)}, s32[4096]{0:T(1024)}, u32[]{:S(2)}) copy-start(s32[4096]{0:T(1024)} %param.15) | copy-start | bytes 49156
  0.0 41.8 %copy-start.5 = (f32[4]{0:T(128)S(1)}, f32[4]{0:T(128)}, u32[]{:S(2)}) copy-start(f32[4]{0:T(128)} %param.14) | copy-start | bytes 52
  1.1 42.0 %copy-start = (f32[2,48,384]{2,1,0:T(8,128)S(1)}, f32[2,48,384]{2,1,0:T(8,128)}, u32[]{:S(2)}) copy-start(f32[2,48,384]{2,1,0:T(8,128)} %constant.109.clone.t2a) | copy-start | bytes 442372
  1.1 41.9 %copy-start.1 = (f32[96,96]{1,0:T(8,128)S(1)}, f32[96,96]{1,0:T(8,128)}, u32[]{:S(2)}) copy-start(f32[96,96]{1,0:T(8,128)} %constant.108.clone.t1) | copy-start | bytes 110596
  1.1 41.9 %copy-start.2 = (f32[2,8,384]{2,1,0:T(8,128)S(1)}, f32[2,8,384]{2,1,0:T(8,128)}, u32[]{:S(2)}) copy-start(f32[2,8,384]{2,1,0:T(8,128)} %constant.110.clone.t2b) | copy-start | bytes 73732
  1.1 41.9 %copy-start.3 = (f32[2,8,384]{2,1,0:T(8,128)S(1)}, f32[2,8,384]{2,1,0:T(8,128)}, u32[]{:S(2)}) copy-start(f32[2,8,384]{2,1,0:T(8,128)} %constant.111.clone.tw) | copy-start | bytes 73732
  1.2 2.0 %collective-permute-start = (f16[112,8,128]{2,1,0:T(8,128)(2,1)S(1)}, f16[112,8,128]{2,1,0:T(8,128)(2,1)S(1)}, u32[]{:S(2)}, u32[]{:S(2)}) collective-permute-start(f16[112,8,128]{2,1,0:T(8,128)(2,1)S(1)} %pad.8), channel_id=1, source_target_pairs={{0,1},{1,0},{2,3},{3,2},{4,5},{5,4},{6,7},{7,6},{8,9},{9,8},{10,11... | collective-permute-start | bytes 688136 | tf_op jit(solution)/shard_map/ppermute | solution.py:223
  41.2 1.5 %collective-permute-start.1 = (f16[112,8,128]{2,1,0:T(8,128)(2,1)S(1)}, f16[112,8,128]{2,1,0:T(8,128)(2,1)S(1)}, u32[]{:S(2)}, u32[]{:S(2)}) collective-permute-start(f16[112,8,128]{2,1,0:T(8,128)(2,1)S(1)} %bitcast.60), channel_id=1, source_target_pairs={{0,1},{1,0},{2,3},{3,2},{4,5},{5,4},{6,7},{7,6},{8,9},{9,8},{10,11... | collective-permute-start | bytes 688136 | tf_op jit(solution)/shard_map/ppermute | solution.py:237
  55.0 1.3 %collective-permute-start.2 = (bf16[20,8,128]{2,1,0:T(8,128)(2,1)S(1)}, bf16[20,8,128]{2,1,0:T(8,128)(2,1)S(1)}, u32[]{:S(2)}, u32[]{:S(2)}) collective-permute-start(bf16[20,8,128]{2,1,0:T(8,128)(2,1)S(1)} %pad_maximum_fusion.2), channel_id=1, source_target_pairs={{0,1},{1,0},{2,3},{3,2},{4,5},{5,4},{6,7},{7,6},{8,9},{9,8},{10,11... | collective-permute-start | bytes 122888 | tf_op jit(solution)/shard_map/ppermute | solution.py:253

commit v8 on v7

--- a/solution.py
+++ b/solution.py
@@ -82,7 +82,7 @@
 
 
 def pairs_kernel(
-    word_any, c_any, v_ref, scale_ref, t1, t2a, t2b, tw, spot_ref, out_ref,
+    word_any, c_any, re_ref, im_ref, scale_ref, t1, t2a, t2b, tw, spot_ref, out_ref,
     word, c_ref, a1, b2, p3, l2, grid, hots, wide, sems, word_sem,
 ):
     def fetch(band):
@@ -104,8 +104,8 @@
                     p = []
                     for yb in range(YB):
                         lanes = slice(yb * SLAB + lt * 128, yb * SLAB + lt * 128 + 128)
-                        v0 = v_ref[0, xs, lanes]
-                        v1 = v_ref[1, xs, lanes]
+                        v0 = re_ref[xs, lanes]
+                        v1 = im_ref[xs, lanes]
                         c0 = c_ref[2 * step + bb, 0, xs, lanes]
                         c1 = c_ref[2 * step + bb, 1, xs, lanes]
                         p.append((v0 * c0 + v1 * c1, v0 * c1 - v1 * c0))
@@ -146,10 +146,16 @@
     ones = jnp.ones((16, 128), BF)
 
     word_copy.wait()
+    def one_hot(b):
+        spots = jnp.broadcast_to(spot_ref[b:b + 1, :], (128, 128)).T
+        hots[b % 2] = (spots == lane).astype(F32)
+
+    one_hot(0)
     for b in range(spot_ref.shape[0]):
         hot = hots.at[b % 2]
-        hot[...] = (jnp.broadcast_to(spot_ref[b:b + 1, :], (128, 128)).T == lane).astype(F32)
         for j in range(4):
+            if j == 1 and b + 1 < spot_ref.shape[0]:
+                one_hot(b + 1)
             rows = []
             for i in range(32 * j, 32 * j + 32):
                 start = pl.multiple_of(word[b * 128 + i], 8)
@@ -175,7 +181,7 @@
     return pl.pallas_call(
         pairs_kernel,
         out_shape=jax.ShapeDtypeStruct((rows, 128), BF),
-        in_specs=[hbm, hbm] + [vmem] * 7,
+        in_specs=[hbm, hbm] + [vmem] * 8,
         out_specs=vmem,
         scratch_shapes=[
             pltpu.SMEM((count,), jnp.int32),
@@ -192,7 +198,7 @@
         ],
         compiler_params=pltpu.CompilerParams(vmem_limit_bytes=40 << 20),
         name="pairs",
-    )(words, cond, valence, scale, *tables(), spots)
+    )(words, cond, *valence, scale, *tables(), spots)
 
 
 def gather_words(gvec_index):
@@ -235,8 +241,10 @@
     half = lax.all_to_all(again, "col", 0, 0, tiled=True, axis_index_groups=groups).reshape(112, 8, 128)
     half, cond_energy, valence_energy = lax.optimization_barrier((half, cond_energy, valence_energy))
     other = lax.ppermute(half, "col", swap)
-    both = jnp.stack([jnp.where(core == 0, half, other), jnp.where(core == 0, other, half)], 0)
-    valence = both[:, :108].reshape(2, 6, 18, 8, 128).transpose(0, 1, 3, 2, 4).reshape(2, L, L * L).astype(F32)
+    def plain(block):
+        return block[:108].reshape(6, 18, 8, 128).transpose(0, 2, 1, 3).reshape(L, L * L).astype(F32)
+
+    valence = plain(jnp.where(core == 0, half, other)), plain(jnp.where(core == 0, other, half))
 
     total_bands = cond_bands.shape[0] * n_col * n_val
     constant = total_bands ** (-0.25) * L ** (-1.5)
@@ -267,7 +275,7 @@
     part = part.reshape(n_val, ROW_DEV, 256).astype(BF)
     summands = lax.all_to_all(part, "val", 0, 0, tiled=True)
     total = jnp.sum(summands.astype(F32), 0)
-    return total.reshape(ROW_DEV, 2, 128).transpose(1, 0, 2)
+    return jnp.stack([total[:, :128], total[:, 128:]], 0)
 
 
 def solution(mesh):

time: 86.7 us -> 86.6 us (level)
  no operation moved by 1% of the time
where the time goes in v8:
time: 86.6 us; the launch traced here: 86.3 us
  blocking collectives  66.5 us (77%)
  Pallas kernels  11.9 us (14%)
  other arithmetic  4.12 us (5%)
  waiting for transfers between devices  1.89 us (2%)
  between operations  0.91 us (1%)
    all_to_all x1, blocking collectives, local(): lax.all_to_all(half.reshape(chips, 7, 8, 128), 'col', 0, 0, tiled=True, a...  22.6 us
    all_to_all x1, blocking collectives, local(): lax.all_to_all(sent, 'col', 0, 0, tiled=True, axis_index_groups=groups)  17.3 us
    all_to_all x1, blocking collectives, local(): lax.all_to_all(again, 'col', 0, 0, tiled=True, axis_index_groups=groups)  15.1 us
    pallas_call x1, Pallas kernels, pair_elements(): pl.pallas_call(pairs_kernel, out_shape=jax.ShapeDtypeStruct((rows, 128),...  11.9 us
    all_to_all x1, blocking collectives, local(): summands = lax.all_to_all(part, 'val', 0, 0, tiled=True)  11.5 us
    convert_element_type x2, other arithmetic, component(): lax.dynamic_index_in_dim(tiles, index, 0, False).astype(jnp.float16)  2.2 us
  transfers between devices with their start and end apart: 3, of which 2 were waited for; matrix products, arithmetic and copies ran while one was open for 2% of the time, Pallas kernels for 0%

profile of v8, /device:TPU:32, one launch (start us, length us, event | category | flops | bytes accessed | tf_op | source)
XLA Modules:
  0.0 86.3 jit_solution(5222441337060539075)
XLA Ops:
  0.0 0.0 copy-start.1
  0.0 0.0 copy-start
  0.0 0.0 copy-start.2
  0.0 0.0 copy-start.3
  0.0 0.0 copy-start.4
  0.0 0.0 copy-start.5
  0.0 1.2 %fusion.3 = f16[108,8,128]{2,1,0:T(8,128)(2,1)S(1)} fusion(f32[2,108,8,128]{3,2,1,0:T(8,128)} %bitcast.67, s32[]{:T(128)S(6)} %select_n.69), kind=kLoop, calls=%fused_computation.13 | loop fusion | flops 110592 | bytes 663556 | tf_op jit(solution)/shard_map/convert_element_type | solution.py:224
  1.3 0.1 collective-permute-start
  1.4 0.7 select_reduce_fusion
  2.1 1.1 %fusion.2 = f16[108,8,128]{2,1,0:T(8,128)(2,1)S(1)} fusion(f32[2,108,8,128]{3,2,1,0:T(8,128)} %bitcast.68, s32[]{:T(128)S(6)} %select_n.68), kind=kLoop, calls=%fused_computation.12 | loop fusion | flops 110592 | bytes 663556 | tf_op jit(solution)/shard_map/convert_element_type | solution.py:224
  3.3 0.0 collective-permute-done
  3.3 0.1 broadcast_select_fusion
  3.4 22.6 %all_to_all.20 = f16[16,7,8,128]{3,2,1,0:T(8,128)(2,1)S(1)} all-to-all(f16[16,7,8,128]{3,2,1,0:T(8,128)(2,1)S(1)} %bitcast.64), channel_id=1, replica_groups={{0,2,4,6,8,10,12,14,16,18,20,22,24,26,28,30},{1,3,5,7,9,11,13,15,17,19,..., dimensions={0} | all-to-all | bytes 458752 | tf_op jit(solution)/shard_map/all_to_all | solution.py:235
  25.9 0.1 convert_reduce_fusion.1
  26.0 0.0 copy-done.4
  26.0 0.1 fusion.17
  26.1 15.1 %all_to_all.21 = f16[16,7,8,128]{3,2,1,0:T(8,128)(2,1)S(1)} all-to-all(f16[16,7,8,128]{3,2,1,0:T(8,128)(2,1)S(1)} %broadcast_in_dim.79), channel_id=1, replica_groups={{0,2,4,6,8,10,12,14,16,18,20,22,24,26,28,30},{1,3,5,7,9,11,13,15,17,19,..., dimensions={0} | all-to-all | bytes 458752 | tf_op jit(solution)/shard_map/all_to_all | solution.py:241
  41.2 0.0 collective-permute-start.1
  41.9 0.0 copy-done.5
  41.9 0.8 collective-permute-done.1
  42.7 0.1 broadcast_select_fusion.1
  42.8 0.1 convert_bitcast_fusion
  42.9 0.1 broadcast_in_dim.80.scale_ref
  43.0 0.0 copy-done.1
  43.0 0.0 copy-done
  43.0 0.0 copy-done.2
  43.0 0.0 copy-done.3
  43.0 11.9 %pairs.1 = bf16[256,128]{1,0:T(8,128)(2,1)S(1)} custom-call(s32[4096]{0:T(1024)S(1)} %get-tuple-element.19.word_any, f32[4,2,48,2304]{3,2,1,0:T(8,128)} %c_any.1, f32[48,2304]{1,0:T(8,128)S(1)} %get-tuple-element.36.re_ref, f32[48,2304]{1,0:T(8,128)S(1)} %get-tuple-element.35.im_ref, f32[4,128]{1,0:T(4,128)S(1)} %broadcast_in_dim.80.scale_ref, ...), custom_call_target="tpu_custom_call" | custom-call | tf_op jit(solution)/shard_map/pairs/pallas_call | solution.py:181
  55.0 0.2 collective-permute-start.2
  55.2 1.1 %collective-permute-done.2 = bf16[20,8,128]{2,1,0:T(8,128)(2,1)S(1)} collective-permute-done((bf16[20,8,128]{2,1,0:T(8,128)(2,1)S(1)}, bf16[20,8,128]{2,1,0:T(8,128)(2,1)S(1)}, u32[]{:S(2)}, u32[]{:S(2)}) %collective-permute-start.2) | collective-permute-done | bytes 40992 | tf_op jit(solution)/shard_map/ppermute | solution.py:261
  56.4 17.3 %all_to_all.22 = bf16[16,10,8,128]{3,2,1,0:T(8,128)(2,1)S(1)} all-to-all(bf16[16,10,8,128]{3,2,1,0:T(8,128)(2,1)S(1)} %pad_maximum_fusion), channel_id=1, replica_groups={{0,2,4,6,8,10,12,14,16,18,20,22,24,26,28,30},{1,3,5,7,9,11,13,15,17,19,..., dimensions={0} | all-to-all | bytes 655360 | tf_op jit(solution)/shard_map/all_to_all | solution.py:266
  73.8 0.3 fusion.1
  74.1 11.5 %all_to_all.23 = bf16[8,64,256]{2,1,0:T(8,128)(2,1)S(1)} all-to-all(bf16[8,64,256]{2,1,0:T(8,128)(2,1)S(1)} %bitcast.71), channel_id=1, replica_groups=mesh['val'=8,'col'=32] {'val'}, dimensions={0} | all-to-all | bytes 524288 | tf_op jit(solution)/shard_map/all_to_all | solution.py:276
  85.7 0.6 pad_maximum_fusion.1
  (23 shorter events, 0.4 us)
Async XLA Ops:
  0.0 43.0 %copy-start.1 = (f32[96,96]{1,0:T(8,128)S(1)}, f32[96,96]{1,0:T(8,128)}, u32[]{:S(2)}) copy-start(f32[96,96]{1,0:T(8,128)} %constant.108.clone.t1) | copy-start | bytes 110596
  0.0 43.0 %copy-start = (f32[2,48,384]{2,1,0:T(8,128)S(1)}, f32[2,48,384]{2,1,0:T(8,128)}, u32[]{:S(2)}) copy-start(f32[2,48,384]{2,1,0:T(8,128)} %constant.109.clone.t2a) | copy-start | bytes 442372
  0.0 43.0 %copy-start.2 = (f32[2,8,384]{2,1,0:T(8,128)S(1)}, f32[2,8,384]{2,1,0:T(8,128)}, u32[]{:S(2)}) copy-start(f32[2,8,384]{2,1,0:T(8,128)} %constant.110.clone.t2b) | copy-start | bytes 73732
  0.0 43.0 %copy-start.3 = (f32[2,8,384]{2,1,0:T(8,128)S(1)}, f32[2,8,384]{2,1,0:T(8,128)}, u32[]{:S(2)}) copy-start(f32[2,8,384]{2,1,0:T(8,128)} %constant.111.clone.tw) | copy-start | bytes 73732
  0.0 26.0 %copy-start.4 = (s32[4096]{0:T(1024)S(1)}, s32[4096]{0:T(1024)}, u32[]{:S(2)}) copy-start(s32[4096]{0:T(1024)} %param.15) | copy-start | bytes 49156
  0.0 41.9 %copy-start.5 = (f32[4]{0:T(128)S(1)}, f32[4]{0:T(128)}, u32[]{:S(2)}) copy-start(f32[4]{0:T(128)} %param.14) | copy-start | bytes 52
  1.3 2.0 %collective-permute-start = (f16[112,8,128]{2,1,0:T(8,128)(2,1)S(1)}, f16[112,8,128]{2,1,0:T(8,128)(2,1)S(1)}, u32[]{:S(2)}, u32[]{:S(2)}) collective-permute-start(f16[112,8,128]{2,1,0:T(8,128)(2,1)S(1)} %pad.8), channel_id=1, source_target_pairs={{0,1},{1,0},{2,3},{3,2},{4,5},{5,4},{6,7},{7,6},{8,9},{9,8},{10,11... | collective-permute-start | bytes 688136 | tf_op jit(solution)/shard_map/ppermute | solution.py:229
  41.2 1.5 %collective-permute-start.1 = (f16[112,8,128]{2,1,0:T(8,128)(2,1)S(1)}, f16[112,8,128]{2,1,0:T(8,128)(2,1)S(1)}, u32[]{:S(2)}, u32[]{:S(2)}) collective-permute-start(f16[112,8,128]{2,1,0:T(8,128)(2,1)S(1)} %bitcast.65), channel_id=1, source_target_pairs={{0,1},{1,0},{2,3},{3,2},{4,5},{5,4},{6,7},{7,6},{8,9},{9,8},{10,11... | collective-permute-start | bytes 688136 | tf_op jit(solution)/shard_map/ppermute | solution.py:243
  55.0 1.3 %collective-permute-start.2 = (bf16[20,8,128]{2,1,0:T(8,128)(2,1)S(1)}, bf16[20,8,128]{2,1,0:T(8,128)(2,1)S(1)}, u32[]{:S(2)}, u32[]{:S(2)}) collective-permute-start(bf16[20,8,128]{2,1,0:T(8,128)(2,1)S(1)} %pad_maximum_fusion.2), channel_id=1, source_target_pairs={{0,1},{1,0},{2,3},{3,2},{4,5},{5,4},{6,7},{7,6},{8,9},{9,8},{10,11... | collective-permute-start | bytes 122888 | tf_op jit(solution)/shard_map/ppermute | solution.py:261
